TPU v7x, 256 devices: a whole 4x4x8 slice. The times are simulated.
256 devices in a mesh: seq: 16 (over z, x_hi), tp: 16 (over y, x_lo, core).
Axes of the slice: x: 4 (x_hi: 2, x_lo: 2; x = x_hi * 2 + x_lo), y: 4, z: 8, core: 2. Of those that a mesh axis runs over, the one named last changes fastest.
Arguments:
- inputs: bfloat16 [8192, 2048], P('seq', 'tp'), may hold values from -6 to 6
- kernel: bfloat16 [8192, 2048], P('seq', 'tp'), may hold values from -6 to 6
- first_blocks: bfloat16 [8192, 512], P('seq'), may hold values from -0.25 to 0.25
- first_cross: bfloat16 [512, 256], P('seq'), may hold values from -1.5 to 1.5
- second_cross: bfloat16 [512, 256], P('seq'), may hold values from -1.5 to 1.5
- second_blocks: bfloat16 [8192, 512], P('seq'), may hold values from -0.25 to 0.25
- gate_weight: bfloat16 [2048, 8192], P('seq', 'tp'), may hold values from -0.125 to 0.125
- up_weight: bfloat16 [2048, 8192], P('seq', 'tp'), may hold values from -0.125 to 0.125
- down_weight: bfloat16 [8192, 2048], P('tp', 'seq'), may hold values from -0.0625 to 0.0625
- cotangent: bfloat16 [8192, 2048], P('seq', 'tp'), may hold values from -6 to 6
Outputs:
- output: bfloat16 [8192, 2048], P('seq', 'tp')
- grad_inputs: bfloat16 [8192, 2048], P('seq', 'tp')
- grad_kernel: bfloat16 [8192, 2048], P('seq', 'tp')
- grad_gate: bfloat16 [2048, 8192], P('seq', 'tp')
- grad_up: bfloat16 [2048, 8192], P('seq', 'tp')
- grad_down: bfloat16 [8192, 2048], P('tp', 'seq')
All inputs are finite; a program needn't handle non-finite values.
Results may differ from a plain program's by a relative error of at most 0.025.
Values may be sent and summed in bfloat16 or wider, within the bound.
A program may use at most 64 MiB of HBM per device.

v0:
```python
import math

import jax
import jax.numpy as jnp
from jax import lax
from jax.sharding import PartitionSpec as P


def swap_blocks(blocks):
    return lax.all_to_all(blocks, "seq", split_axis=0, concat_axis=0, tiled=True)


def fetch_weights(gate_weight, up_weight, down_weight):
    return (
        lax.all_gather(gate_weight, "seq", axis=0, tiled=True),
        lax.all_gather(up_weight, "seq", axis=0, tiled=True),
        lax.all_gather(down_weight, "seq", axis=1, tiled=True),
    )


def per_device(
    inputs,
    kernel,
    first_blocks,
    first_cross,
    second_cross,
    second_blocks,
    gate_weight,
    up_weight,
    down_weight,
    cotangent,
):
    groups = lax.axis_size("seq")
    length, channels = inputs.shape
    stride = length // groups
    cross_one = first_cross.reshape(stride, groups, groups)
    cross_two = second_cross.reshape(stride, groups, groups)
    inner_mix = jnp.dot(first_blocks, inputs, preferred_element_type=jnp.float32).astype(
        jnp.bfloat16
    )
    spread = swap_blocks(inner_mix.reshape(groups, stride, channels))
    crossed = jnp.einsum(
        "tqp,ptc->qtc", cross_one, spread, preferred_element_type=jnp.float32
    ).astype(jnp.bfloat16)
    crossed_home = swap_blocks(crossed).reshape(length, channels)
    scaled = (kernel.astype(jnp.float32) * crossed_home.astype(jnp.float32)).astype(jnp.bfloat16)
    scaled_out = swap_blocks(scaled.reshape(groups, stride, channels))
    mixed_out = jnp.einsum(
        "tuq,qtc->utc", cross_two, scaled_out, preferred_element_type=jnp.float32
    ).astype(jnp.bfloat16)
    mixed_home = swap_blocks(mixed_out).reshape(length, channels)
    branch = jnp.dot(second_blocks, mixed_home, preferred_element_type=jnp.float32)
    hidden_in = (inputs.astype(jnp.float32) + branch).astype(jnp.bfloat16)
    features = lax.all_gather(hidden_in, "tp", axis=1, tiled=True)
    gate_full, up_full, down_full = fetch_weights(gate_weight, up_weight, down_weight)
    gate_proj = jnp.dot(features, gate_full, preferred_element_type=jnp.float32)
    up_proj = jnp.dot(features, up_full, preferred_element_type=jnp.float32)
    sig_gate = jax.nn.sigmoid(gate_proj)
    hidden = (gate_proj * sig_gate * up_proj).astype(jnp.bfloat16)
    down_terms = jnp.dot(hidden, down_full, preferred_element_type=jnp.float32)
    down_sum = lax.psum_scatter(
        down_terms.astype(jnp.bfloat16), "tp", scatter_dimension=1, tiled=True
    ).astype(jnp.float32)
    output = (hidden_in.astype(jnp.float32) + down_sum).astype(jnp.bfloat16)
    gate_full, up_full, down_full = fetch_weights(gate_weight, up_weight, down_weight)
    full_cot = lax.all_gather(cotangent, "tp", axis=1, tiled=True)
    back_hidden = jnp.einsum("sd,fd->sf", full_cot, down_full, preferred_element_type=jnp.float32)
    back_gate = (back_hidden * up_proj * sig_gate * (1.0 + gate_proj * (1.0 - sig_gate))).astype(
        jnp.bfloat16
    )
    back_up = (back_hidden * gate_proj * sig_gate).astype(jnp.bfloat16)
    back_terms = jnp.einsum("sf,df->sd", back_gate, gate_full, preferred_element_type=jnp.float32)
    back_terms = back_terms + jnp.einsum(
        "sf,df->sd", back_up, up_full, preferred_element_type=jnp.float32
    )
    back_total = cotangent.astype(jnp.float32) + lax.psum_scatter(
        back_terms.astype(jnp.bfloat16), "tp", scatter_dimension=1, tiled=True
    ).astype(jnp.float32)
    grad_scale = 1.0 / math.sqrt(length * groups)
    term_gate = (
        jnp.einsum("sd,sf->df", features, back_gate, preferred_element_type=jnp.float32)
        * grad_scale
    )
    term_up = (
        jnp.einsum("sd,sf->df", features, back_up, preferred_element_type=jnp.float32) * grad_scale
    )
    term_down = (
        jnp.einsum("sf,sd->fd", hidden, full_cot, preferred_element_type=jnp.float32) * grad_scale
    )
    sum_gate, sum_up, sum_down = (
        lax.psum_scatter(
            term_gate.astype(jnp.bfloat16), "seq", scatter_dimension=0, tiled=True
        ).astype(jnp.float32),
        lax.psum_scatter(
            term_up.astype(jnp.bfloat16), "seq", scatter_dimension=0, tiled=True
        ).astype(jnp.float32),
        lax.psum_scatter(
            term_down.astype(jnp.bfloat16), "seq", scatter_dimension=1, tiled=True
        ).astype(jnp.float32),
    )
    back_branch = back_total.astype(jnp.bfloat16)
    back_mixed = jnp.einsum(
        "st,sc->tc", second_blocks, back_branch, preferred_element_type=jnp.float32
    ).astype(jnp.bfloat16)
    back_spread = swap_blocks(back_mixed.reshape(groups, stride, channels))
    back_scaled = jnp.einsum(
        "tuq,utc->qtc", cross_two, back_spread, preferred_element_type=jnp.float32
    ).astype(jnp.bfloat16)
    back_home = swap_blocks(back_scaled).reshape(length, channels)
    grad_kernel = (back_home.astype(jnp.float32) * crossed_home.astype(jnp.float32)).astype(
        jnp.bfloat16
    )
    back_crossed = (back_home.astype(jnp.float32) * kernel.astype(jnp.float32)).astype(jnp.bfloat16)
    crossed_out = swap_blocks(back_crossed.reshape(groups, stride, channels))
    back_inner = jnp.einsum(
        "tqp,qtc->ptc", cross_one, crossed_out, preferred_element_type=jnp.float32
    ).astype(jnp.bfloat16)
    inner_home = swap_blocks(back_inner).reshape(length, channels)
    back_source = jnp.einsum(
        "ts,tc->sc", first_blocks, inner_home, preferred_element_type=jnp.float32
    )
    grad_inputs = (back_total + back_source).astype(jnp.bfloat16)
    return (
        output,
        grad_inputs,
        grad_kernel,
        sum_gate.astype(jnp.bfloat16),
        sum_up.astype(jnp.bfloat16),
        sum_down.astype(jnp.bfloat16),
    )


def solution(mesh):
    return jax.shard_map(
        per_device,
        mesh=mesh,
        in_specs=(
            P("seq", "tp"),
            P("seq", "tp"),
            P("seq", None),
            P("seq", None),
            P("seq", None),
            P("seq", None),
            P("seq", "tp"),
            P("seq", "tp"),
            P("tp", "seq"),
            P("seq", "tp"),
        ),
        out_specs=(
            P("seq", "tp"),
            P("seq", "tp"),
            P("seq", "tp"),
            P("seq", "tp"),
            P("seq", "tp"),
            P("tp", "seq"),
        ),
        check_vma=False,
    )
```

profile of v0, /device:TPU:1, one launch (start us, length us, event | category | flops | bytes accessed | tf_op | source)
XLA Modules:
  0.0 1127.7 jit_solution(15990717286811365970)
XLA Ops:
  10.0 11.6 %all-to-all-start = ((bf16[16,32,128]{2,1,0:T(8,128)(2,1)}), bf16[16,32,128]{2,1,0:T(8,128)(2,1)S(1)}, u32[]{:S(2)}, u32[]{:S(2)}) async-start(bf16[16,32,128]{2,1,0:T(8,128)(2,1)} %bitcast), calls=%async_computation | async-start | bytes 262144 | tf_op jit(solution)/shard_map/all_to_all | solution.py:10
  22.6 9.0 all-to-all-done
  31.9 13.2 %all_to_all.40 = bf16[16,32,128]{2,1,0:T(8,128)(2,1)S(1)} all-to-all(bf16[16,32,128]{2,1,0:T(8,128)(2,1)S(1)} %copy.47), channel_id=1, replica_groups=mesh['seq'=16,'tp'=16] {'seq'}, dimensions={0} | all-to-all | bytes 262144 | tf_op jit(solution)/shard_map/all_to_all | solution.py:10
  45.8 3.5 all-to-all-start.2
  49.7 9.8 all-to-all-done.2
  60.4 3.5 all-to-all-start.3
  64.1 10.5 all-to-all-done.3
  77.6 20.9 %all-gather.10.cloned.1.call-done = bf16[2048,512]{1,0:T(8,128)(2,1)} async-done(((bf16[128,512]{1,0:T(8,128)(2,1)}), bf16[2048,512]{1,0:T(8,128)(2,1)}) %all-gather.10.cloned.1.call-update) | async-done | bytes 2097168 | tf_op jit(solution)/shard_map/all_gather | solution.py:16
  98.5 39.4 %all-gather.6.cloned.1.call-done = bf16[512,2048]{0,1:T(8,128)(2,1)} async-done(((bf16[512,128]{0,1:T(8,128)(2,1)}), bf16[512,2048]{0,1:T(8,128)(2,1)}) %all-gather.6.cloned.1.call-update) | async-done | bytes 2097168 | tf_op jit(solution)/shard_map/all_gather | solution.py:54
  137.9 4.7 fusion.20
  142.5 79.6 %all-gather.8.cloned.1.call-done = bf16[2048,512]{1,0:T(8,128)(2,1)} async-done(((bf16[128,512]{1,0:T(8,128)(2,1)}), bf16[2048,512]{1,0:T(8,128)(2,1)}) %all-gather.8.cloned.1.call-update) | async-done | bytes 2097168 | tf_op jit(solution)/shard_map/all_gather | solution.py:15
  222.1 3.8 fusion.19
  225.9 80.7 %all-gather.12.cloned.1.call-done = bf16[512,2048]{1,0:T(8,128)(2,1)} async-done(((bf16[512,128]{1,0:T(8,128)(2,1)}), bf16[512,2048]{1,0:T(8,128)(2,1)}) %all-gather.12.cloned.1.call-update) | async-done | bytes 2097168 | tf_op jit(solution)/shard_map/all_gather | solution.py:17
  306.6 41.5 %all-gather.14.cloned.1.call-done = bf16[512,2048]{1,0:T(8,128)(2,1)} async-done(((bf16[512,128]{1,0:T(8,128)(2,1)}), bf16[512,2048]{1,0:T(8,128)(2,1)}) %all-gather.14.cloned.1.call-update) | async-done | bytes 2097168 | tf_op jit(solution)/shard_map/all_gather | solution.py:66
  348.1 5.3 multiply_convert_fusion.3
  366.3 3.7 convolution_convert_fusion
  378.9 44.2 %reduce-scatter.16.cloned.1.call-done = bf16[128,512]{1,0:T(8,128)(2,1)} async-done(((bf16[2048,512]{1,0:T(8,128)(2,1)}), bf16[128,512]{1,0:T(8,128)(2,1)}) %reduce-scatter.16.cloned.1.call-update) | async-done | bytes 131088
  424.4 19.0 %all_to_all.41 = bf16[16,32,128]{2,1,0:T(8,128)(2,1)S(1)} all-to-all(bf16[16,32,128]{2,1,0:T(8,128)(2,1)S(1)} %bitcast.80), channel_id=1, replica_groups=mesh['seq'=16,'tp'=16] {'seq'}, dimensions={0} | all-to-all | bytes 262144 | tf_op jit(solution)/shard_map/all_to_all | solution.py:10
  443.7 12.5 %all_to_all.42 = bf16[16,32,128]{2,1,0:T(8,128)(2,1)S(1)} all-to-all(bf16[16,32,128]{2,1,0:T(8,128)(2,1)S(1)} %copy.58), channel_id=1, replica_groups=mesh['seq'=16,'tp'=16] {'seq'}, dimensions={0} | all-to-all | bytes 262144 | tf_op jit(solution)/shard_map/all_to_all | solution.py:10
  456.9 12.6 %all_to_all.43 = bf16[16,32,128]{2,1,0:T(8,128)(2,1)S(1)} all-to-all(bf16[16,32,128]{2,1,0:T(8,128)(2,1)S(1)} %bitcast.79), channel_id=1, replica_groups=mesh['seq'=16,'tp'=16] {'seq'}, dimensions={0} | all-to-all | bytes 262144 | tf_op jit(solution)/shard_map/all_to_all | solution.py:10
  474.0 158.6 %reduce-scatter.18.cloned.1.call-done = bf16[128,512]{1,0:T(8,128)(2,1)} async-done(((bf16[2048,512]{1,0:T(8,128)(2,1)}), bf16[128,512]{1,0:T(8,128)(2,1)}) %reduce-scatter.18.cloned.1.call-update) | async-done | bytes 131088
  634.2 67.9 %reduce-scatter.10.cloned.1.call-done = bf16[512,128]{0,1:T(8,128)(2,1)} async-done(((bf16[512,2048]{0,1:T(8,128)(2,1)}), bf16[512,128]{0,1:T(8,128)(2,1)}) %reduce-scatter.10.cloned.1.call-update) | async-done | bytes 131088 | tf_op jit(solution)/shard_map/reduce_scatter | solution.py:61
  704.9 205.9 %reduce-scatter.12.cloned.1.call-done = bf16[128,512]{1,0:T(8,128)(2,1)} async-done(((bf16[2048,512]{1,0:T(8,128)(2,1)}), bf16[128,512]{1,0:T(8,128)(2,1)}) %reduce-scatter.12.cloned.1.call-update) | async-done | bytes 131088 | tf_op jit(solution)/shard_map/reduce_scatter | solution.py:91
  910.8 210.0 %reduce-scatter.14.cloned.1.call-done = bf16[128,512]{1,0:T(8,128)(2,1)} async-done(((bf16[2048,512]{1,0:T(8,128)(2,1)}), bf16[128,512]{1,0:T(8,128)(2,1)}) %reduce-scatter.14.cloned.1.call-update) | async-done | bytes 131088 | tf_op jit(solution)/shard_map/reduce_scatter | solution.py:94
  (86 shorter events, 41.8 us)
Async XLA Ops:
  7.2 67.5 %copy-start = (bf16[512,512]{1,0:T(8,128)(2,1)S(1)}, bf16[512,512]{1,0:T(8,128)(2,1)}, u32[]{:S(2)}) copy-start(bf16[512,512]{1,0:T(8,128)(2,1)} %param.15) | copy-start | bytes 1572868
  7.2 38.0 %copy-start.7 = (bf16[512,128]{1,0:T(8,128)(2,1)S(1)}, bf16[512,128]{1,0:T(8,128)(2,1)}, u32[]{:S(2)}) copy-start(bf16[512,128]{1,0:T(8,128)(2,1)} %param.11) | copy-start | bytes 393220
  7.2 42.2 %copy-start.12 = (bf16[32,256]{1,0:T(8,128)(2,1)S(1)}, bf16[32,256]{1,0:T(8,128)(2,1)}, u32[]{:S(2)}) copy-start(bf16[32,256]{1,0:T(8,128)(2,1)} %param.14) | copy-start | bytes 49156
  7.2 91.3 %all-gather.10.cloned.1.call-start = ((), (), s32[]{:S(2)}) async-start(), calls=%async_computation.15 | async-start | bytes 2228224 | tf_op jit(solution)/shard_map/all_gather | solution.py:16
  7.2 56.7 %copy-start.10 = (bf16[512,128]{1,0:T(8,128)(2,1)S(1)}, bf16[512,128]{1,0:T(8,128)(2,1)}, u32[]{:S(2)}) copy-start(bf16[512,128]{1,0:T(8,128)(2,1)} %param.10) | copy-start | bytes 393220
  10.0 21.7 %all-to-all-start = ((bf16[16,32,128]{2,1,0:T(8,128)(2,1)}), bf16[16,32,128]{2,1,0:T(8,128)(2,1)S(1)}, u32[]{:S(2)}, u32[]{:S(2)}) async-start(bf16[16,32,128]{2,1,0:T(8,128)(2,1)} %bitcast), calls=%async_computation | async-start | bytes 262144 | tf_op jit(solution)/shard_map/all_to_all | solution.py:10
  45.8 13.6 %all-to-all-start.2 = ((bf16[16,32,128]{2,1,0:T(8,128)(2,1)}), bf16[16,32,128]{2,1,0:T(8,128)(2,1)S(1)}, u32[]{:S(2)}, u32[]{:S(2)}) async-start(bf16[16,32,128]{2,1,0:T(8,128)(2,1)} %bitcast.4), calls=%async_computation.2 | async-start | bytes 262144 | tf_op jit(solution)/shard_map/all_to_all | solution.py:10
  60.4 14.2 %all-to-all-start.3 = ((bf16[16,32,128]{2,1,0:T(8,128)(2,1)}), bf16[16,32,128]{2,1,0:T(8,128)(2,1)S(1)}, u32[]{:S(2)}, u32[]{:S(2)}) async-start(bf16[16,32,128]{2,1,0:T(8,128)(2,1)} %copy.51), calls=%async_computation.3 | async-start | bytes 262144 | tf_op jit(solution)/shard_map/all_to_all | solution.py:10
  63.9 73.9 %all-gather.6.cloned.1.call-start = ((), (), s32[]{:S(2)}) async-start(), calls=%async_computation.13 | async-start | bytes 2228224 | tf_op jit(solution)/shard_map/all_gather | solution.py:54
  75.6 146.5 %all-gather.8.cloned.1.call-start = ((), (), s32[]{:S(2)}) async-start(), calls=%async_computation.14 | async-start | bytes 2228224 | tf_op jit(solution)/shard_map/all_gather | solution.py:15
  76.4 230.3 %all-gather.12.cloned.1.call-start = ((), (), s32[]{:S(2)}) async-start(), calls=%async_computation.16 | async-start | bytes 2228224 | tf_op jit(solution)/shard_map/all_gather | solution.py:17
  76.9 271.2 %all-gather.14.cloned.1.call-start = ((), (), s32[]{:S(2)}) async-start(), calls=%async_computation.18 | async-start | bytes 2228224 | tf_op jit(solution)/shard_map/all_gather | solution.py:66
  77.5 345.6 %reduce-scatter.16.cloned.1.call-start = ((), (), s32[]{:S(2)}) async-start(), calls=%async_computation.21 | async-start | bytes 2228224
  137.8 84.2 %copy-start.13 = (bf16[512,2048]{0,1:T(8,128)(2,1)S(1)}, bf16[512,2048]{0,1:T(8,128)(2,1)}, u32[]{:S(2)}) copy-start(bf16[512,2048]{0,1:T(8,128)(2,1)} %all-gather.6.cloned.1.call-done) | copy-start | bytes 6291460
  225.9 127.5 %copy-start.3 = (bf16[2048,512]{1,0:T(8,128)(2,1)S(1)}, bf16[2048,512]{1,0:T(8,128)(2,1)}, u32[]{:S(2)}) copy-start(bf16[2048,512]{1,0:T(8,128)(2,1)} %all-gather.8.cloned.1.call-done) | copy-start | bytes 6291460
  359.0 273.5 %reduce-scatter.18.cloned.1.call-start = ((), (), s32[]{:S(2)}) async-start(), calls=%async_computation.22 | async-start | bytes 2228224
  364.7 337.4 %reduce-scatter.10.cloned.1.call-start = ((), (), s32[]{:S(2)}) async-start(), calls=%async_computation.17 | async-start | bytes 2228224 | tf_op jit(solution)/shard_map/reduce_scatter | solution.py:61
  370.0 540.8 %reduce-scatter.12.cloned.1.call-start = ((), (), s32[]{:S(2)}) async-start(), calls=%async_computation.19 | async-start | bytes 2228224 | tf_op jit(solution)/shard_map/reduce_scatter | solution.py:91
  374.2 746.6 %reduce-scatter.14.cloned.1.call-start = ((), (), s32[]{:S(2)}) async-start(), calls=%async_computation.20 | async-start | bytes 2228224 | tf_op jit(solution)/shard_map/reduce_scatter | solution.py:94
  377.9 78.3 %copy-start.8 = (bf16[512,128]{1,0:T(8,128)(2,1)S(1)}, bf16[512,128]{1,0:T(8,128)(2,1)}, u32[]{:S(2)}) copy-start(bf16[512,128]{1,0:T(8,128)(2,1)} %param.11) | copy-start | bytes 393220
  378.9 323.3 %copy-start.4 = (bf16[512,128]{0,1:T(8,128)(2,1)S(1)}, bf16[512,128]{0,1:T(8,128)(2,1)}, u32[]{:S(2)}) copy-start(bf16[512,128]{0,1:T(8,128)(2,1)} %fusion.2) | copy-start | bytes 393220
  424.3 279.6 %copy-start.2 = (bf16[512,512]{1,0:T(8,128)(2,1)S(1)}, bf16[512,512]{1,0:T(8,128)(2,1)}, u32[]{:S(2)}) copy-start(bf16[512,512]{1,0:T(8,128)(2,1)} %param.12) | copy-start | bytes 1572868
  424.3 279.6 %copy-start.11 = (bf16[128,512]{1,0:T(8,128)(2,1)S(1)}, bf16[128,512]{1,0:T(8,128)(2,1)}, u32[]{:S(2)}) copy-start(bf16[128,512]{1,0:T(8,128)(2,1)} %reduce-scatter.16.cloned.1.call-done) | copy-start | bytes 393220
  470.5 233.4 %all-to-all-start.7 = ((bf16[16,32,128]{2,1,0:T(8,128)(2,1)}), bf16[16,32,128]{2,1,0:T(8,128)(2,1)S(1)}, u32[]{:S(2)}, u32[]{:S(2)}) async-start(bf16[16,32,128]{2,1,0:T(8,128)(2,1)} %copy.61), calls=%async_computation.8 | async-start | bytes 262144 | tf_op jit(solution)/shard_map/all_to_all | solution.py:10
  (6 other events, 8.3 us)
Sparse Core Ops, SparseCore 0:
  10.6 87.7 all-gather.9
  100.9 36.9 all-gather.5
  140.4 81.5 all-gather.7
  224.4 82.1 all-gather.11
  308.3 39.8 all-gather.13
  359.2 63.9 reduce-scatter.15
  427.0 205.4 reduce-scatter.17
  635.1 67.0 reduce-scatter.9
  706.6 204.1 reduce-scatter.11
  915.1 205.6 reduce-scatter.13
where the time goes:
time: 1130 us
  waiting for transfers between devices  981 us (87%)
  blocking collectives  57.4 us (5%)
  matrix products  33.5 us (3%)
  starting transfers between devices  22.7 us (2%)
  local copies, waits for them, and re-layouts  16.7 us (1%)
  between operations  14.4 us (1%)
    reduce_scatter x1, waiting for transfers between devices, per_device(): lax.psum_scatter(term_up.astype(jnp.bfloat16), 'seq', scatter_dimension=0...  210 us
    reduce_scatter x1, waiting for transfers between devices, per_device(): lax.psum_scatter(term_gate.astype(jnp.bfloat16), 'seq', scatter_dimension...  206 us
    unnamed x12, waiting for transfers between devices  205 us
    all_gather x1, waiting for transfers between devices, fetch_weights(): lax.all_gather(down_weight, 'seq', axis=1, tiled=True)  80.7 us
    all_gather x1, waiting for transfers between devices, fetch_weights(): lax.all_gather(gate_weight, 'seq', axis=0, tiled=True)  79.6 us
    reduce_scatter x1, waiting for transfers between devices, per_device(): lax.psum_scatter(down_terms.astype(jnp.bfloat16), 'tp', scatter_dimension...  67.9 us
    all_to_all x4, blocking collectives, swap_blocks(): lax.all_to_all(blocks, 'seq', split_axis=0, concat_axis=0, tiled=True)  57.4 us
    all_gather x1, waiting for transfers between devices, per_device(): full_cot = lax.all_gather(cotangent, 'tp', axis=1, tiled=True)  41.5 us
  transfers between devices with their start and end apart: 14, of which 13 were waited for; matrix products, arithmetic and copies ran while one was open for 3% of the time, Pallas kernels for 0%

commit v1 on v0

v1 whole, which is shorter than its diff:
```python
import math

import jax
import jax.numpy as jnp
from jax import lax
from jax.experimental import pallas as pl
from jax.experimental.pallas import tpu as pltpu
from jax.sharding import PartitionSpec as P

MESH = pl.DeviceIdType.MESH
BF = jnp.bfloat16
F32 = jnp.float32
MIB = 1 << 20
N_SEM = 512


def dot(a, b):
    return jnp.dot(a, b, preferred_element_type=F32)


def dot_nt(a, b):
    return lax.dot_general(a, b, (((1,), (1,)), ((), ())), preferred_element_type=F32)


def rem(a, n):
    return lax.rem(a, jnp.int32(n))


def div(a, n):
    return lax.div(a, jnp.int32(n))


def mo(v, n):
    return pl.multiple_of(v, n)


def layer_kernel(
    x, kk, a1, c1, c2, a2, wg, wu, wd, cot,
    out, grad_in, grad_k, o_gate, o_up, o_down,
    wgf, wuf, wdf, feat, cotf,
    m1, m1t, m2, m2t, a1t, a2t,
    inner, spread, kspread, crossed, mixed, mhome, hid_in,
    bh, hidden, bgate, bup, bt, dt,
    gg, gu, gd, coregot, rsum,
    zr, swap_src, swap_got, r1, r2, r3, r4, rhome, total,
    bmix, bspread, gks, binner, ihome, gkhome,
    ssem, rsem,
):
    s = lax.axis_index("seq")
    t = lax.axis_index("tp")
    z, h = div(s, 2), rem(s, 2)
    y, l, c = div(t, 4), rem(div(t, 2), 2), rem(t, 2)
    xx = h * 2 + l
    own_side = c == h

    def seq_dev(j):
        return {"seq": j, "tp": t}

    def z_dev(d):
        return {"seq": rem(z + (8 + d), 8) * 2 + h, "tp": t}

    def plane(yy, xp):
        return {"seq": z * 2 + div(xp, 2), "tp": yy * 4 + rem(xp, 2) * 2 + c}

    core_dev = {"seq": s, "tp": t + 1 - 2 * c}
    swap_dev = {"seq": z * 2 + 1 - h, "tp": t + 1 - 2 * c}

    def nb(axis, d):
        if axis == "y":
            return plane(rem(y + (4 + d), 4), xx)
        return plane(y, rem(xx + (4 + d), 4))

    count = [0]
    sends = []

    def remote(src, dst, dev):
        i = count[0]
        count[0] += 1
        return pltpu.make_async_remote_copy(
            src, dst, ssem.at[i], rsem.at[i], device_id=dev, device_id_type=MESH
        )

    def send(src, dst, dev):
        copy = remote(src, dst, dev)
        copy.start()
        sends.append(copy.wait_send)
        return copy

    def exchange_order(i):
        k = div(i + 1, 2)
        return 8 + k * (2 * rem(i + 1, 2) - 1)

    def exchange(src, dst):
        base = count[0]
        count[0] += 15

        def copy(i):
            j = rem(s + exchange_order(i), 16)
            return pltpu.make_async_remote_copy(
                src.at[pl.ds(mo(j * 32, 32), 32)],
                dst.at[pl.ds(mo(s * 32, 32), 32)],
                ssem.at[base + i], rsem.at[base + i],
                device_id=seq_dev(j), device_id_type=MESH,
            )

        def over(act):
            def step(i, carry):
                act(copy(i))
                return carry
            lax.fori_loop(0, 15, step, 0)

        over(lambda p: p.start())
        mine = pl.ds(mo(s * 32, 32), 32)
        dst[mine, :] = src[mine, :]
        sends.append(lambda: over(lambda p: p.wait_send()))
        return lambda: over(lambda p: p.wait_recv())

    def slot(ref, a, first, f, g, r0, nr):
        yy, xp = (f, g) if first == "y" else (g, f)
        rows = div(xp, 2) * 256 + (a * 128 + r0)
        cols = (yy * 2 + rem(xp, 2)) * 256
        return ref.at[pl.ds(mo(rows, 64), nr), pl.ds(mo(cols, 256), 256)]

    def axes_of(first):
        return (y, xx, "x") if first == "y" else (xx, y, "y")

    def gather_plane(buf):
        halves = ((0, "y"), (1, "x"))
        st1, st2 = {}, {}

        def second(a, first, di):
            p1, p2, other = axes_of(first)
            f = rem(p1 + (4 + di), 4)
            piece = slot(buf, a, first, f, p2, 0, 128)
            st2[a, di] = [send(piece, piece, nb(other, d)) for d in (1, -1)]

        def second_forward(a, first, di):
            p1, p2, other = axes_of(first)
            f = rem(p1 + (4 + di), 4)
            got = []
            for k, d in ((0, 1), (1, -1)):
                st2[a, di][k].wait_recv()
                piece = slot(buf, a, first, f, rem(p2 + (4 - d), 4), k * 64, 64)
                got.append(send(piece, piece, nb(other, d)))
            st2[a, di] = got

        for a, first in halves:
            p1, p2, _ = axes_of(first)
            piece = slot(buf, a, first, p1, p2, 0, 128)
            st1[a] = [send(piece, piece, nb(first, d)) for d in (1, -1)]
        for a, first in halves:
            second(a, first, 0)
        yield
        fwd = {}
        for a, first in halves:
            p1, p2, _ = axes_of(first)
            fwd[a] = []
            for k, d in ((0, 1), (1, -1)):
                st1[a][k].wait_recv()
                piece = slot(buf, a, first, rem(p1 + (4 - d), 4), p2, k * 64, 64)
                fwd[a].append(send(piece, piece, nb(first, d)))
        for a, first in halves:
            second(a, first, -1)
            second(a, first, 1)
        yield
        for a, first in halves:
            second_forward(a, first, 0)
        yield
        for a, first in halves:
            for copy in fwd[a]:
                copy.wait_recv()
            second(a, first, 2)
        yield
        for di in (-1, 1):
            for a, first in halves:
                second_forward(a, first, di)
        yield
        for a, first in halves:
            second_forward(a, first, 2)
        yield
        for di in (0, -1, 1, 2):
            for a, first in halves:
                for copy in st2[a, di]:
                    copy.wait_recv()

    def add_into(ref, *others):
        value = ref[...].astype(F32)
        for other in others:
            value = value + other[...].astype(F32)
        ref[...] = value.astype(BF)

    def scatter_plane(buf, w):
        halves = ((0, "x"), (1, "y"))
        order = (2, 1, -1, 0)
        st1, st2, st3, st4 = {}, {}, {}, {}
        for gi, dg in enumerate(order):
            for a, first in halves:
                p1, p2, _ = axes_of(first)
                f, g = rem(p1 + 2, 4), rem(p2 + (4 + dg), 4)
                st1[a, gi] = [
                    send(
                        slot(buf, a, first, f, g, k * 64, 64), r1.at[w, a, gi, k], nb(first, d)
                    )
                    for k, d in ((0, 1), (1, -1))
                ]
        yield
        for gi, dg in enumerate(order):
            for a, first in halves:
                p1, p2, _ = axes_of(first)
                g = rem(p2 + (4 + dg), 4)
                st2[a, gi] = []
                for k, d in ((0, 1), (1, -1)):
                    st1[a, gi][k].wait_recv()
                    f = rem(p1 + (4 + d), 4)
                    add_into(slot(buf, a, first, f, g, k * 64, 64), r1.at[w, a, gi, k])
                    st2[a, gi].append(
                        send(
                            slot(buf, a, first, f, g, 0, 128), r2.at[w, a, gi, k], nb(first, d)
                        )
                    )
            yield
        for gi, dg in enumerate(order):
            for a, first in halves:
                p1, p2, other = axes_of(first)
                g = rem(p2 + (4 + dg), 4)
                for copy in st2[a, gi]:
                    copy.wait_recv()
                add_into(
                    slot(buf, a, first, p1, g, 0, 128), r2.at[w, a, gi, 0], r2.at[w, a, gi, 1]
                )
                if dg == 2:
                    st3[a] = [
                        send(
                            slot(buf, a, first, p1, g, k * 64, 64), r3.at[w, a, k], nb(other, d)
                        )
                        for k, d in ((0, 1), (1, -1))
                    ]
            yield
        for a, first in halves:
            p1, p2, other = axes_of(first)
            st4[a] = []
            for k, d in ((0, 1), (1, -1)):
                g = rem(p2 + (4 + d), 4)
                st3[a][k].wait_recv()
                add_into(slot(buf, a, first, p1, g, k * 64, 64), r3.at[w, a, k])
                st4[a].append(
                    send(slot(buf, a, first, p1, g, 0, 128), r4.at[w, a, k], nb(other, d))
                )
        yield
        for a, first in halves:
            p1, p2, other = axes_of(first)
            for copy in st4[a]:
                copy.wait_recv()
            add_into(slot(buf, a, first, p1, p2, 0, 128), r4.at[w, a, 0], r4.at[w, a, 1])
        rows = pl.ds(mo(h * 256, 256), 256)
        cols = pl.ds(mo((y * 2 + l) * 256 + (1 - c) * 128, 128), 128)
        back = send(buf.at[rows, cols], rhome.at[w], core_dev)
        yield
        back.wait_recv()

    half_rows = pl.ds(mo(c * 256, 256), 256)
    other_rows = pl.ds(mo((1 - c) * 256, 256), 256)
    my_rows = pl.ds(mo(h * 256, 256), 256)
    my_cols = pl.ds(mo((y * 2 + l) * 256 + c * 128, 128), 128)

    def share_core(src, buf):
        copy = send(src.at[other_rows], buf.at[my_rows, my_cols], core_dev)
        buf[my_rows, my_cols] = src[half_rows, :]
        return copy

    def wslice(w, j, part=None):
        ref = (wdf, wgf, wuf)[w]
        if w == 0:
            rows = pl.ds(0, 512) if part is None else pl.ds(part * 256, 256)
            return ref.at[rows, pl.ds(mo(j * 128, 128), 128)]
        if part is None:
            return ref.at[pl.ds(mo(j * 128, 128), 128), :]
        return ref.at[pl.ds(mo(j * 128 + part * 64, 64), 64), :]

    wsrc = (wd, wg, wu)
    core_waits = []

    def ring_weights():
        swaps = [remote(wsrc[w], wslice(w, s), swap_dev) for w in range(3)]

        @pl.when(jnp.logical_not(own_side))
        def _():
            for copy in swaps:
                copy.start()

        @pl.when(own_side)
        def _():
            for w in range(3):
                wslice(w, s)[...] = wsrc[w][...]

        def wait_swaps():
            @pl.when(jnp.logical_not(own_side))
            def _():
                for copy in swaps:
                    copy.wait_send()

        sends.append(wait_swaps)
        yield
        pend = {}

        def pass_on(w, dz, d, part=None):
            piece = wslice(w, rem(z + (8 + dz), 8) * 2 + c, part)
            pend[w, d] = send(piece, piece, z_dev(d))

        def to_core(w, dz):
            piece = wslice(w, rem(z + (8 + dz), 8) * 2 + c)
            core_waits.append(send(piece, piece, core_dev))

        for w in range(3):
            @pl.when(jnp.logical_not(own_side))
            def _():
                swaps[w].wait_recv()
            pass_on(w, 0, 1)
            pass_on(w, 0, -1)
        for w in range(3):
            to_core(w, 0)
        yield
        for k in (1, 2, 3):
            for w in range(3):
                for d in (1, -1):
                    pend[w, d].wait_recv()
                    part = None if k < 3 else (0 if d == 1 else 1)
                    pass_on(w, -d * k, d, part)
                for d in (1, -1):
                    to_core(w, -d * k)
                yield
        for w in range(3):
            for d in (1, -1):
                pend[w, d].wait_recv()
            to_core(w, 4)
        yield
        for copy in core_waits:
            copy.wait_recv()

    def core_blocks(w, buf):
        return [buf, w]

    gbufs = (gg, gu, gd)
    got_core = {}
    zorder = (4, 3, -3, 2, -2, 1, -1, 0)

    def grad_tiles(w, lhs, rhs, scale):
        lhs_t = lhs[...].T
        for i, dz in enumerate(zorder):
            zz = rem(z + (8 + dz), 8)
            cols = pl.ds(mo(zz * 256, 256), 256)
            gbufs[w][:, cols] = (dot(lhs_t, rhs[:, cols]) * scale).astype(BF)
            there = pl.ds(mo(zz * 256 + (1 - c) * 128, 128), 128)
            got_core[w, i] = send(gbufs[w].at[:, there], coregot.at[w, i], core_dev)

    def mine_block(w, dz, part=None):
        zz = rem(z + (8 + dz), 8)
        cols = pl.ds(mo(zz * 256 + c * 128, 128), 128)
        rows = pl.ds(0, 512) if part is None else pl.ds(part * 256, 256)
        return gbufs[w].at[rows, cols]

    def ring_grads(w):
        for i in (0,):
            got_core[w, i].wait_recv()
            add_into(mine_block(w, 4), coregot.at[w, i])
        pend = [
            send(mine_block(w, 4, k), zr.at[w, 0, k, pl.ds(0, 256)], z_dev(d))
            for k, d in ((0, 1), (1, -1))
        ]
        for i in range(1, 8):
            got_core[w, i].wait_recv()
            add_into(mine_block(w, zorder[i]), coregot.at[w, i])
        yield
        for n in (3, 2, 1):
            new = []
            for k, d in ((0, 1), (1, -1)):
                pend[k].wait_recv()
                if n == 3:
                    add_into(mine_block(w, d * n, k), zr.at[w, 0, k, pl.ds(0, 256)])
                else:
                    add_into(mine_block(w, d * n), zr.at[w, 3 - n, k])
                new.append(send(mine_block(w, d * n), zr.at[w, 4 - n, k], z_dev(d)))
            pend = new
            yield
        for copy in pend:
            copy.wait_recv()
        add_into(mine_block(w, 0), zr.at[w, 3, 0], zr.at[w, 3, 1])
        swap = remote(mine_block(w, 0), swap_got.at[w], swap_dev)

        @pl.when(jnp.logical_not(own_side))
        def _():
            swap.start()

        yield

        @pl.when(jnp.logical_not(own_side))
        def _():
            swap.wait()

        @pl.when(own_side)
        def _():
            swap_got[w] = mine_block(w, 0)[...]

        if w == 0:
            o_gate[...] = swap_got[w].T
        elif w == 1:
            o_up[...] = swap_got[w].T
        else:
            o_down[...] = swap_got[w]

    def run(flow, n=1):
        for _ in range(n):
            next(flow, None)

    def drain(flow):
        for _ in flow:
            pass

    barrier = pltpu.get_barrier_semaphore()
    partners = [seq_dev(rem(s + d, 16)) for d in range(1, 16)]
    partners += [nb("y", 1), nb("y", -1), nb("x", 1), nb("x", -1), core_dev, swap_dev]
    for dev in partners:
        pl.semaphore_signal(barrier, inc=1, device_id=dev, device_id_type=MESH)
    inner[...] = dot(a1[...], x[...]).astype(BF)
    pl.semaphore_wait(barrier, len(partners))

    got_inner = exchange(inner, spread)
    got_k = exchange(kk, kspread)
    weights = ring_weights()
    run(weights)
    got_cot = share_core(cot, cotf)

    row = lax.broadcasted_iota(jnp.int32, (256, 512), 0)
    col = lax.broadcasted_iota(jnp.int32, (256, 512), 1)
    pick = (row == div(col, 32)).astype(F32).astype(BF)
    pick_t = (row == div(col, 32) * 16).astype(F32).astype(BF)
    diag = (
        lax.broadcasted_iota(jnp.int32, (32, 512), 0)
        == rem(lax.broadcasted_iota(jnp.int32, (32, 512), 1), 32)
    ).astype(F32)

    def widen(cross, m, mt):
        values = cross[...].astype(F32)

        def step(i, carry):
            rows = pl.ds(mo(i * 32, 32), 32)
            turned = pltpu.roll(values, 256 - i * 16, 1).astype(BF)
            m[rows, :] = (dot(turned, pick) * diag).astype(BF)
            turned = pltpu.roll(values, 256 - i, 1).astype(BF)
            mt[rows, :] = (dot(turned, pick_t) * diag).astype(BF)
            return carry

        lax.fori_loop(0, 16, step, 0)

    widen(c1, m1, m1t)
    widen(c2, m2, m2t)

    got_cot.wait_recv()
    cot_flow = gather_plane(cotf)
    run(cot_flow)

    got_inner()
    crossed[...] = dot(m1[...], spread[...]).astype(BF)
    got_k()
    scaled = (kspread[...].astype(F32) * crossed[...].astype(F32)).astype(BF)
    mixed[...] = dot(m2[...], scaled).astype(BF)
    got_mixed = exchange(mixed, mhome)
    a1t[...] = a1[...].T
    a2t[...] = a2[...].T
    run(weights)
    run(cot_flow, 2)
    got_mixed()
    hid_in[...] = (x[...].astype(F32) + dot(a2[...], mhome[...])).astype(BF)
    got_feat = share_core(hid_in, feat)
    run(cot_flow)
    got_feat.wait_recv()
    feat_flow = gather_plane(feat)
    run(feat_flow)
    run(weights, 3)
    run(cot_flow)
    run(feat_flow)
    run(cot_flow)
    run(feat_flow)
    drain(cot_flow)
    run(weights, 3)
    run(feat_flow)
    run(weights, 3)
    run(feat_flow)
    run(weights)
    drain(weights)
    for j in range(2):
        cols = pl.ds(j * 256, 256)
        bh[:, cols] = dot_nt(cotf[...], wdf[cols, :])
    drain(feat_flow)

    for j in range(2):
        cols = pl.ds(j * 256, 256)
        gate = dot(feat[...], wgf[:, cols])
        up = dot(feat[...], wuf[:, cols])
        sig = 1.0 / (1.0 + jnp.exp(-gate))
        back = bh[:, cols]
        hidden[:, cols] = (gate * sig * up).astype(BF)
        bgate[:, cols] = (back * up * sig * (1.0 + gate * (1.0 - sig))).astype(BF)
        bup[:, cols] = (back * gate * sig).astype(BF)
    for j in range(8):
        rows = pl.ds(j * 256, 256)
        bt[:, rows] = (dot_nt(bgate[...], wgf[rows, :]) + dot_nt(bup[...], wuf[rows, :])).astype(BF)
    back_flow = scatter_plane(bt, 0)
    run(back_flow)
    scale = 1.0 / math.sqrt(8192.0)
    grad_tiles(0, bgate, feat, scale)
    run(back_flow, 4)
    grads = [ring_grads(w) for w in range(3)]
    run(grads[0])
    grad_tiles(1, bup, feat, scale)
    run(back_flow, 4)
    run(grads[1])
    grad_tiles(2, hidden, cotf, scale)
    run(back_flow)
    run(grads[0])
    run(grads[2])
    run(back_flow)
    for j in range(8):
        cols = pl.ds(j * 256, 256)
        dt[:, cols] = dot(hidden[...], wdf[:, cols]).astype(BF)
    drain(back_flow)
    down_flow = scatter_plane(dt, 1)
    run(down_flow)

    total[half_rows, :] = cot[half_rows, :].astype(F32) + bt[my_rows, my_cols].astype(F32)
    total[other_rows, :] = cot[other_rows, :].astype(F32) + rhome[0].astype(F32)
    bmix[...] = dot(a2t[...], total[...].astype(BF)).astype(BF)
    got_back = exchange(bmix, bspread)
    for w in (1, 0, 2, 1):
        run(grads[w])
    run(down_flow, 4)
    got_back()
    bscaled = dot(m2t[...], bspread[...]).astype(BF).astype(F32)
    bcrossed = (bscaled * kspread[...].astype(F32)).astype(BF)
    gks[...] = (bscaled * crossed[...].astype(F32)).astype(BF)
    binner[...] = dot(m1t[...], bcrossed).astype(BF)
    got_binner = exchange(binner, ihome)
    got_gk = exchange(gks, gkhome)
    for w in (0, 2, 1):
        run(grads[w])
    run(down_flow, 4)
    for w in (0, 2):
        run(grads[w])
    got_binner()
    grad_in[...] = (total[...] + dot(a1t[...], ihome[...])).astype(BF)
    run(down_flow)
    got_gk()
    grad_k[...] = gkhome[...]
    run(down_flow)
    for w in (0, 1, 2):
        run(grads[w])
    drain(down_flow)
    out[half_rows, :] = (
        hid_in[half_rows, :].astype(F32) + dt[my_rows, my_cols].astype(F32)
    ).astype(BF)
    out[other_rows, :] = (hid_in[other_rows, :].astype(F32) + rhome[1].astype(F32)).astype(BF)
    for w in (0, 1, 2):
        drain(grads[w])
    for wait in sends:
        wait()
    assert count[0] <= N_SEM, count[0]


def per_device(*args):
    vm = pltpu.VMEM
    scratch = [
        vm((2048, 512), BF), vm((2048, 512), BF), vm((512, 2048), BF),
        vm((512, 2048), BF), vm((512, 2048), BF),
    ]
    scratch += [vm((512, 512), BF)] * 6
    scratch += [vm((512, 128), BF)] * 7
    scratch += [vm((512, 512), F32)] + [vm((512, 512), BF)] * 3
    scratch += [vm((512, 2048), BF)] * 2
    scratch += [vm((512, 2048), BF)] * 3
    scratch += [vm((3, 8, 512, 128), BF), vm((16, 128), BF)]
    scratch += [
        vm((3, 4, 2, 512, 128), BF), vm((16, 128), BF), vm((3, 512, 128), BF),
        vm((2, 2, 4, 2, 64, 256), BF), vm((2, 2, 4, 2, 128, 256), BF),
        vm((2, 2, 2, 64, 256), BF), vm((2, 2, 2, 128, 256), BF),
        vm((2, 256, 128), BF), vm((512, 128), F32),
    ]
    scratch += [vm((512, 128), BF)] * 6
    scratch += [pltpu.SemaphoreType.DMA((N_SEM,)), pltpu.SemaphoreType.DMA((N_SEM,))]
    wide = jax.ShapeDtypeStruct((512, 128), BF)
    tall = jax.ShapeDtypeStruct((128, 512), BF)
    return pl.pallas_call(
        layer_kernel,
        name="mixer_layer",
        out_shape=[wide, wide, wide, tall, tall, wide],
        in_specs=[pl.BlockSpec(memory_space=vm)] * 10,
        out_specs=[pl.BlockSpec(memory_space=vm)] * 6,
        scratch_shapes=scratch,
        compiler_params=pltpu.CompilerParams(
            collective_id=0, has_side_effects=True, vmem_limit_bytes=56 * MIB
        ),
    )(*args)


def solution(mesh):
    return jax.shard_map(
        per_device,
        mesh=mesh,
        in_specs=(
            P("seq", "tp"),
            P("seq", "tp"),
            P("seq", None),
            P("seq", None),
            P("seq", None),
            P("seq", None),
            P("seq", "tp"),
            P("seq", "tp"),
            P("tp", "seq"),
            P("seq", "tp"),
        ),
        out_specs=(
            P("seq", "tp"),
            P("seq", "tp"),
            P("seq", "tp"),
            P("seq", "tp"),
            P("seq", "tp"),
            P("tp", "seq"),
        ),
        check_vma=False,
    )
```

time: 1130 us -> 147 us (0.13)
  waiting for transfers between devices: 981 us -> 0 us
  Pallas kernels: 0 us -> 140 us
  blocking collectives: 57.4 us -> 0 us
  matrix products: 33.5 us -> 0 us
  starting transfers between devices: 22.7 us -> 0 us
  between operations: 14.4 us -> 0.66 us
    reduce_scatter x3 -> x0, waiting for transfers between devices: 484 us -> none  [the longest x1 210 us: per_device(): lax.psum_scatter(term_up.astype(jnp.bfloat16), 'seq', scatter_dimension=0...]
    all_gather x5 -> x0, waiting for transfers between devices: 262 us -> none  [the longest x1 80.7 us: fetch_weights(): lax.all_gather(down_weight, 'seq', axis=1, tiled=True)]
    unnamed x12 -> x0, waiting for transfers between devices: 205 us -> none
    pallas_call x0 -> x1, Pallas kernels: none -> 140 us  [per_device(): pl.pallas_call(layer_kernel, name='mixer_layer', out_shape=[wide, wide, w...]
    all_to_all x4 -> x0, blocking collectives: 57.4 us -> none  [swap_blocks(): lax.all_to_all(blocks, 'seq', split_axis=0, concat_axis=0, tiled=True)]
    dot_general x17 -> x0, matrix products: 33.5 us -> none  [the longest x1 5.26 us: per_device(): jnp.einsum('sd,fd->sf', full_cot, down_full, preferred_element_type=jnp.f...]
    all_to_all x4 -> x0, waiting for transfers between devices: 29.4 us -> none  [swap_blocks(): lax.all_to_all(blocks, 'seq', split_axis=0, concat_axis=0, tiled=True)]
    all_to_all x4 -> x0, starting transfers between devices: 22.1 us -> none  [swap_blocks(): lax.all_to_all(blocks, 'seq', split_axis=0, concat_axis=0, tiled=True)]
  transfers between devices with their start and end apart: 14 -> 0, of which waited for: 13 -> 0; matrix products, arithmetic and copies ran while one was open for 3% -> 0% of each run, Pallas kernels for 0% -> 0%
where the time goes in v1:
time: 147 us
  Pallas kernels  140 us (95%)
  local copies, waits for them, and re-layouts  6.06 us (4%)
    pallas_call x1, Pallas kernels, per_device(): pl.pallas_call(layer_kernel, name='mixer_layer', out_shape=[wide, wide, w...  140 us
    unnamed x16, local copies, waits for them, and re-layouts  6.06 us

profile of v1, /device:TPU:1, one launch (start us, length us, event | category | flops | bytes accessed | tf_op | source)
XLA Modules:
  0.0 146.7 jit_solution(6821859452030517161)
XLA Ops:
  0.6 140.0 %mixer_layer.1 = (bf16[512,128]{1,0:T(8,128)(2,1)}, bf16[512,128]{1,0:T(8,128)(2,1)}, bf16[512,128]{1,0:T(8,128)(2,1)}, bf16[128,512]{1,0:T(8,128)(2,1)}, bf16[1...) custom-call(bf16[512,128]{1,0:T(8,128)(2,1)} %x.1, bf16[512,128]{1,0:T(8,128)(2,1)} %kk.1, bf16[512,512]{1,0:T(8,128)(2,1)} %a1.1, ...), custom_call_target="tpu_custom_call" | custom-call | tf_op jit(solution)/shard_map/mixer_layer/pallas_call | solution.py:591
  140.6 0.0 copy-start.4
  140.6 1.6 %copy.22 = bf16[512,128]{1,0:T(8,128)(2,1)} copy(bf16[512,128]{1,0:T(8,128)(2,1)} %get-tuple-element.12) | data formatting | bytes 262144
  142.2 0.0 copy-done.4
  142.2 0.0 copy-start.3
  142.2 0.7 copy.23
  142.9 0.3 copy-done.3
  143.2 0.0 copy-start.2
  143.2 0.7 copy.24
  143.8 0.3 copy-done.2
  144.1 0.0 copy-start.1
  144.1 0.7 copy.25
  144.8 0.3 copy-done.1
  145.1 0.0 copy-start
  145.1 0.7 copy.26
  145.8 0.3 copy-done
  146.0 0.7 copy.27
Async XLA Ops:
  140.6 1.6 %copy-start.4 = (bf16[512,128]{1,0:T(8,128)(2,1)S(1)}, bf16[512,128]{1,0:T(8,128)(2,1)}, u32[]{:S(2)}) copy-start(bf16[512,128]{1,0:T(8,128)(2,1)} %get-tuple-element.13) | copy-start | bytes 393220
  142.2 1.0 copy-start.3
  143.2 1.0 copy-start.2
  144.1 1.0 copy-start.1
  145.1 1.0 copy-start

commit v2 on v1

--- a/solution.py
+++ b/solution.py
@@ -41,8 +41,8 @@
     m1, m1t, m2, m2t, a1t, a2t,
     inner, spread, kspread, crossed, mixed, mhome, hid_in,
     bh, hidden, bgate, bup, bt, dt,
-    gg, gu, gd, coregot, rsum,
-    zr, swap_src, swap_got, r1, r2, r3, r4, rhome, total,
+    gg, gu, gd, coregot, turned, lhs_t,
+    zr, swap_got, r1, r2, r3, r4, rhome, total,
     bmix, bspread, gks, binner, ihome, gkhome,
     ssem, rsem,
 ):
@@ -282,6 +282,16 @@
 
     def ring_weights():
         swaps = [remote(wsrc[w], wslice(w, s), swap_dev) for w in range(3)]
+        pend = {}
+        first = {}
+        for w in range(3):
+            piece = wslice(w, z * 2 + c)
+            pend[w, 1] = remote(piece, piece, z_dev(1))
+            pend[w, -1] = remote(piece, piece, z_dev(-1))
+            first[w] = [pend[w, 1], pend[w, -1], remote(piece, piece, core_dev)]
+            for copy in first[w]:
+                sends.append(copy.wait_send)
+            core_waits.append(first[w][2])
 
         @pl.when(jnp.logical_not(own_side))
         def _():
@@ -292,6 +302,8 @@
         def _():
             for w in range(3):
                 wslice(w, s)[...] = wsrc[w][...]
+                for copy in first[w]:
+                    copy.start()
 
         def wait_swaps():
             @pl.when(jnp.logical_not(own_side))
@@ -301,7 +313,6 @@
 
         sends.append(wait_swaps)
         yield
-        pend = {}
 
         def pass_on(w, dz, d, part=None):
             piece = wslice(w, rem(z + (8 + dz), 8) * 2 + c, part)
@@ -311,14 +322,13 @@
             piece = wslice(w, rem(z + (8 + dz), 8) * 2 + c)
             core_waits.append(send(piece, piece, core_dev))
 
-        for w in range(3):
-            @pl.when(jnp.logical_not(own_side))
-            def _():
+        @pl.when(jnp.logical_not(own_side))
+        def _():
+            for w in range(3):
                 swaps[w].wait_recv()
-            pass_on(w, 0, 1)
-            pass_on(w, 0, -1)
-        for w in range(3):
-            to_core(w, 0)
+                for copy in first[w]:
+                    copy.start()
+
         yield
         for k in (1, 2, 3):
             for w in range(3):
@@ -337,20 +347,16 @@
         for copy in core_waits:
             copy.wait_recv()
 
-    def core_blocks(w, buf):
-        return [buf, w]
-
     gbufs = (gg, gu, gd)
     got_core = {}
     zorder = (4, 3, -3, 2, -2, 1, -1, 0)
 
-    def grad_tiles(w, lhs, rhs, scale):
-        lhs_t = lhs[...].T
-        for i, dz in enumerate(zorder):
-            zz = rem(z + (8 + dz), 8)
-            cols = pl.ds(mo(zz * 256, 256), 256)
-            gbufs[w][:, cols] = (dot(lhs_t, rhs[:, cols]) * scale).astype(BF)
-            there = pl.ds(mo(zz * 256 + (1 - c) * 128, 128), 128)
+    def grad_tiles(i):
+        zz = rem(z + (8 + zorder[i]), 8)
+        cols = pl.ds(mo(zz * 256, 256), 256)
+        there = pl.ds(mo(zz * 256 + (1 - c) * 128, 128), 128)
+        for w, rhs in ((0, feat), (1, feat), (2, cotf)):
+            gbufs[w][:, cols] = (dot(lhs_t[w], rhs[:, cols]) * scale).astype(BF)
             got_core[w, i] = send(gbufs[w].at[:, there], coregot.at[w, i], core_dev)
 
     def mine_block(w, dz, part=None):
@@ -359,54 +365,64 @@
         rows = pl.ds(0, 512) if part is None else pl.ds(part * 256, 256)
         return gbufs[w].at[rows, cols]
 
-    def ring_grads(w):
-        for i in (0,):
-            got_core[w, i].wait_recv()
-            add_into(mine_block(w, 4), coregot.at[w, i])
-        pend = [
-            send(mine_block(w, 4, k), zr.at[w, 0, k, pl.ds(0, 256)], z_dev(d))
-            for k, d in ((0, 1), (1, -1))
-        ]
-        for i in range(1, 8):
+    def core_sum(i):
+        for w in range(3):
             got_core[w, i].wait_recv()
             add_into(mine_block(w, zorder[i]), coregot.at[w, i])
+
+    def ring_grads():
+        pend = {}
+        for w in range(3):
+            got_core[w, 0].wait_recv()
+            add_into(mine_block(w, 4), coregot.at[w, 0])
+            pend[w] = [
+                send(mine_block(w, 4, k), zr.at[w, 0, k, pl.ds(0, 256)], z_dev(d))
+                for k, d in ((0, 1), (1, -1))
+            ]
         yield
         for n in (3, 2, 1):
-            new = []
-            for k, d in ((0, 1), (1, -1)):
-                pend[k].wait_recv()
-                if n == 3:
-                    add_into(mine_block(w, d * n, k), zr.at[w, 0, k, pl.ds(0, 256)])
-                else:
-                    add_into(mine_block(w, d * n), zr.at[w, 3 - n, k])
-                new.append(send(mine_block(w, d * n), zr.at[w, 4 - n, k], z_dev(d)))
-            pend = new
+            for w in range(3):
+                new = []
+                for k, d in ((0, 1), (1, -1)):
+                    pend[w][k].wait_recv()
+                    if n == 3:
+                        add_into(mine_block(w, d * n, k), zr.at[w, 0, k, pl.ds(0, 256)])
+                    else:
+                        add_into(mine_block(w, d * n), zr.at[w, 3 - n, k])
+                    new.append(send(mine_block(w, d * n), zr.at[w, 4 - n, k], z_dev(d)))
+                pend[w] = new
+                yield
+        swaps = []
+        for w in range(3):
+            for copy in pend[w]:
+                copy.wait_recv()
+            add_into(mine_block(w, 0), zr.at[w, 3, 0], zr.at[w, 3, 1])
+            swap = remote(mine_block(w, 0), swap_got.at[w], swap_dev)
+            swaps.append(swap)
+
+            @pl.when(jnp.logical_not(own_side))
+            def _():
+                swap.start()
+
             yield
-        for copy in pend:
-            copy.wait_recv()
-        add_into(mine_block(w, 0), zr.at[w, 3, 0], zr.at[w, 3, 1])
-        swap = remote(mine_block(w, 0), swap_got.at[w], swap_dev)
-
-        @pl.when(jnp.logical_not(own_side))
-        def _():
-            swap.start()
-
-        yield
-
-        @pl.when(jnp.logical_not(own_side))
-        def _():
-            swap.wait()
-
-        @pl.when(own_side)
-        def _():
-            swap_got[w] = mine_block(w, 0)[...]
-
-        if w == 0:
-            o_gate[...] = swap_got[w].T
-        elif w == 1:
-            o_up[...] = swap_got[w].T
-        else:
-            o_down[...] = swap_got[w]
+        for w in range(3):
+            swap = swaps[w]
+
+            @pl.when(jnp.logical_not(own_side))
+            def _():
+                swap.wait()
+
+            @pl.when(own_side)
+            def _():
+                swap_got[w] = mine_block(w, 0)[...]
+
+            if w == 0:
+                o_gate[...] = swap_got[w].T
+            elif w == 1:
+                o_up[...] = swap_got[w].T
+            else:
+                o_down[...] = swap_got[w]
+            yield
 
     def run(flow, n=1):
         for _ in range(n):
@@ -416,77 +432,75 @@
         for _ in flow:
             pass
 
+    scale = 1.0 / math.sqrt(8192.0)
     barrier = pltpu.get_barrier_semaphore()
     partners = [seq_dev(rem(s + d, 16)) for d in range(1, 16)]
     partners += [nb("y", 1), nb("y", -1), nb("x", 1), nb("x", -1), core_dev, swap_dev]
     for dev in partners:
         pl.semaphore_signal(barrier, inc=1, device_id=dev, device_id_type=MESH)
     inner[...] = dot(a1[...], x[...]).astype(BF)
-    pl.semaphore_wait(barrier, len(partners))
-
-    got_inner = exchange(inner, spread)
-    got_k = exchange(kk, kspread)
-    weights = ring_weights()
-    run(weights)
-    got_cot = share_core(cot, cotf)
 
     row = lax.broadcasted_iota(jnp.int32, (256, 512), 0)
     col = lax.broadcasted_iota(jnp.int32, (256, 512), 1)
     pick = (row == div(col, 32)).astype(F32).astype(BF)
     pick_t = (row == div(col, 32) * 16).astype(F32).astype(BF)
-    diag = (
-        lax.broadcasted_iota(jnp.int32, (32, 512), 0)
-        == rem(lax.broadcasted_iota(jnp.int32, (32, 512), 1), 32)
-    ).astype(F32)
-
-    def widen(cross, m, mt):
+    diag = rem(lax.broadcasted_iota(jnp.int32, (512, 512), 0), 32) == rem(
+        lax.broadcasted_iota(jnp.int32, (512, 512), 1), 32
+    )
+
+    def widen(cross, m, shift, picked):
         values = cross[...].astype(F32)
-
-        def step(i, carry):
-            rows = pl.ds(mo(i * 32, 32), 32)
-            turned = pltpu.roll(values, 256 - i * 16, 1).astype(BF)
-            m[rows, :] = (dot(turned, pick) * diag).astype(BF)
-            turned = pltpu.roll(values, 256 - i, 1).astype(BF)
-            mt[rows, :] = (dot(turned, pick_t) * diag).astype(BF)
-            return carry
-
-        lax.fori_loop(0, 16, step, 0)
-
-    widen(c1, m1, m1t)
-    widen(c2, m2, m2t)
-
+        for i in range(16):
+            moved = values if i == 0 else pltpu.roll(values, 256 - i * shift, 1)
+            turned[pl.ds(i * 32, 32), :] = moved.astype(BF)
+        m[...] = jnp.where(diag, dot(turned[...], picked), 0.0).astype(BF)
+
+    widen(c1, m1, 16, pick)
+    pl.semaphore_wait(barrier, len(partners))
+
+    got_inner = exchange(inner, spread)
+    weights = ring_weights()
+    run(weights)
+    got_cot = share_core(cot, cotf)
+    got_k = exchange(kk, kspread)
+    widen(c2, m2, 16, pick)
     got_cot.wait_recv()
     cot_flow = gather_plane(cotf)
     run(cot_flow)
-
+    run(weights)
+    a1t[...] = a1[...].T
     got_inner()
     crossed[...] = dot(m1[...], spread[...]).astype(BF)
     got_k()
     scaled = (kspread[...].astype(F32) * crossed[...].astype(F32)).astype(BF)
     mixed[...] = dot(m2[...], scaled).astype(BF)
     got_mixed = exchange(mixed, mhome)
-    a1t[...] = a1[...].T
+    run(cot_flow)
+    run(weights, 3)
     a2t[...] = a2[...].T
-    run(weights)
-    run(cot_flow, 2)
+    run(cot_flow)
+    widen(c1, m1t, 1, pick_t)
+    widen(c2, m2t, 1, pick_t)
+    run(cot_flow)
     got_mixed()
     hid_in[...] = (x[...].astype(F32) + dot(a2[...], mhome[...])).astype(BF)
     got_feat = share_core(hid_in, feat)
-    run(cot_flow)
+    run(weights)
     got_feat.wait_recv()
     feat_flow = gather_plane(feat)
     run(feat_flow)
-    run(weights, 3)
     run(cot_flow)
+    run(weights, 2)
     run(feat_flow)
     run(cot_flow)
+    run(weights, 1)
     run(feat_flow)
     drain(cot_flow)
-    run(weights, 3)
+    run(weights, 1)
     run(feat_flow)
-    run(weights, 3)
+    run(weights, 1)
     run(feat_flow)
-    run(weights)
+    run(feat_flow)
     drain(weights)
     for j in range(2):
         cols = pl.ds(j * 256, 256)
@@ -499,71 +513,86 @@
         up = dot(feat[...], wuf[:, cols])
         sig = 1.0 / (1.0 + jnp.exp(-gate))
         back = bh[:, cols]
-        hidden[:, cols] = (gate * sig * up).astype(BF)
-        bgate[:, cols] = (back * up * sig * (1.0 + gate * (1.0 - sig))).astype(BF)
-        bup[:, cols] = (back * gate * sig).astype(BF)
+        hid = (gate * sig * up).astype(BF)
+        hidden[:, cols] = hid
+        lhs_t[2, cols, :] = hid.T
+        bg = (back * up * sig * (1.0 + gate * (1.0 - sig))).astype(BF)
+        bgate[:, cols] = bg
+        lhs_t[0, cols, :] = bg.T
+        bu = (back * gate * sig).astype(BF)
+        bup[:, cols] = bu
+        lhs_t[1, cols, :] = bu.T
+    grad_tiles(0)
+    grad_tiles(1)
+    grad_tiles(2)
+    grads = ring_grads()
+    run(grads)
     for j in range(8):
         rows = pl.ds(j * 256, 256)
         bt[:, rows] = (dot_nt(bgate[...], wgf[rows, :]) + dot_nt(bup[...], wuf[rows, :])).astype(BF)
     back_flow = scatter_plane(bt, 0)
     run(back_flow)
-    scale = 1.0 / math.sqrt(8192.0)
-    grad_tiles(0, bgate, feat, scale)
-    run(back_flow, 4)
-    grads = [ring_grads(w) for w in range(3)]
-    run(grads[0])
-    grad_tiles(1, bup, feat, scale)
-    run(back_flow, 4)
-    run(grads[1])
-    grad_tiles(2, hidden, cotf, scale)
+    core_sum(1)
+    core_sum(2)
+    for i in range(3, 8):
+        grad_tiles(i)
+    run(grads)
     run(back_flow)
-    run(grads[0])
-    run(grads[2])
+    run(grads)
     run(back_flow)
+    run(grads)
+    run(back_flow, 2)
+    for i in range(3, 8):
+        core_sum(i)
+    run(back_flow, 2)
+    run(grads)
+    run(back_flow, 2)
+    run(grads)
     for j in range(8):
         cols = pl.ds(j * 256, 256)
         dt[:, cols] = dot(hidden[...], wdf[:, cols]).astype(BF)
+    run(back_flow)
+    run(grads)
     drain(back_flow)
-    down_flow = scatter_plane(dt, 1)
-    run(down_flow)
-
     total[half_rows, :] = cot[half_rows, :].astype(F32) + bt[my_rows, my_cols].astype(F32)
     total[other_rows, :] = cot[other_rows, :].astype(F32) + rhome[0].astype(F32)
     bmix[...] = dot(a2t[...], total[...].astype(BF)).astype(BF)
     got_back = exchange(bmix, bspread)
-    for w in (1, 0, 2, 1):
-        run(grads[w])
+    down_flow = scatter_plane(dt, 1)
+    run(down_flow)
+    run(grads)
     run(down_flow, 4)
+    run(grads)
     got_back()
     bscaled = dot(m2t[...], bspread[...]).astype(BF).astype(F32)
     bcrossed = (bscaled * kspread[...].astype(F32)).astype(BF)
-    gks[...] = (bscaled * crossed[...].astype(F32)).astype(BF)
     binner[...] = dot(m1t[...], bcrossed).astype(BF)
     got_binner = exchange(binner, ihome)
+    gks[...] = (bscaled * crossed[...].astype(F32)).astype(BF)
     got_gk = exchange(gks, gkhome)
-    for w in (0, 2, 1):
-        run(grads[w])
-    run(down_flow, 4)
-    for w in (0, 2):
-        run(grads[w])
+    run(grads)
+    run(down_flow, 5)
+    run(grads)
+    run(down_flow)
     got_binner()
     grad_in[...] = (total[...] + dot(a1t[...], ihome[...])).astype(BF)
-    run(down_flow)
+    run(grads)
     got_gk()
     grad_k[...] = gkhome[...]
-    run(down_flow)
-    for w in (0, 1, 2):
-        run(grads[w])
     drain(down_flow)
     out[half_rows, :] = (
         hid_in[half_rows, :].astype(F32) + dt[my_rows, my_cols].astype(F32)
     ).astype(BF)
     out[other_rows, :] = (hid_in[other_rows, :].astype(F32) + rhome[1].astype(F32)).astype(BF)
-    for w in (0, 1, 2):
-        drain(grads[w])
+    drain(grads)
     for wait in sends:
         wait()
     assert count[0] <= N_SEM, count[0]
+
+
+def hand_over(*refs):
+    for i in range(6):
+        refs[6 + i][...] = refs[i][...]
 
 
 def per_device(*args):
@@ -577,9 +606,9 @@
     scratch += [vm((512, 512), F32)] + [vm((512, 512), BF)] * 3
     scratch += [vm((512, 2048), BF)] * 2
     scratch += [vm((512, 2048), BF)] * 3
-    scratch += [vm((3, 8, 512, 128), BF), vm((16, 128), BF)]
+    scratch += [vm((3, 8, 512, 128), BF), vm((512, 256), BF), vm((3, 512, 512), BF)]
     scratch += [
-        vm((3, 4, 2, 512, 128), BF), vm((16, 128), BF), vm((3, 512, 128), BF),
+        vm((3, 4, 2, 512, 128), BF), vm((3, 512, 128), BF),
         vm((2, 2, 4, 2, 64, 256), BF), vm((2, 2, 4, 2, 128, 256), BF),
         vm((2, 2, 2, 64, 256), BF), vm((2, 2, 2, 128, 256), BF),
         vm((2, 256, 128), BF), vm((512, 128), F32),
@@ -588,7 +617,7 @@
     scratch += [pltpu.SemaphoreType.DMA((N_SEM,)), pltpu.SemaphoreType.DMA((N_SEM,))]
     wide = jax.ShapeDtypeStruct((512, 128), BF)
     tall = jax.ShapeDtypeStruct((128, 512), BF)
-    return pl.pallas_call(
+    results = pl.pallas_call(
         layer_kernel,
         name="mixer_layer",
         out_shape=[wide, wide, wide, tall, tall, wide],
@@ -599,6 +628,13 @@
             collective_id=0, has_side_effects=True, vmem_limit_bytes=56 * MIB
         ),
     )(*args)
+    return pl.pallas_call(
+        hand_over,
+        name="hand_over",
+        out_shape=[wide, wide, wide, tall, tall, wide],
+        in_specs=[pl.BlockSpec(memory_space=vm)] * 6,
+        out_specs=[pl.BlockSpec(memory_space=vm)] * 6,
+    )(*results)
 
 
 def solution(mesh):

time: 147 us -> 127 us (0.86)
  Pallas kernels: 140 us -> 125 us
  local copies, waits for them, and re-layouts: 6.06 us -> 0 us
    pallas_call x1, Pallas kernels: 140 us -> 123 us  [per_device(): pl.pallas_call(layer_kernel, name='mixer_layer', out_shape=[wide, wide, w...]
    unnamed x16 -> x0, local copies, waits for them, and re-layouts: 6.06 us -> none
    pallas_call x0 -> x1, Pallas kernels: none -> 2.09 us  [per_device(): pl.pallas_call(hand_over, name='hand_over', out_shape=[wide, wide, wide,...]
where the time goes in v2:
time: 127 us; the launch traced here: 126 us
  Pallas kernels  125 us (98%)
    pallas_call x1, Pallas kernels, per_device(): pl.pallas_call(layer_kernel, name='mixer_layer', out_shape=[wide, wide, w...  123 us

profile of v2, /device:TPU:1, one launch (start us, length us, event | category | flops | bytes accessed | tf_op | source)
XLA Modules:
  0.0 126.1 jit_solution(3887024013214733550)
XLA Ops:
  0.6 123.3 %mixer_layer.1 = (bf16[512,128]{1,0:T(8,128)(2,1)}, bf16[512,128]{1,0:T(8,128)(2,1)}, bf16[512,128]{1,0:T(8,128)(2,1)}, bf16[128,512]{1,0:T(8,128)(2,1)}, bf16[1...) custom-call(bf16[512,128]{1,0:T(8,128)(2,1)} %x.1, bf16[512,128]{1,0:T(8,128)(2,1)} %kk.1, bf16[512,512]{1,0:T(8,128)(2,1)} %a1.1, ...), custom_call_target="tpu_custom_call" | custom-call | tf_op jit(solution)/shard_map/mixer_layer/pallas_call | solution.py:620
  124.0 2.1 %hand_over.1 = (bf16[512,128]{1,0:T(8,128)(2,1)}, bf16[512,128]{1,0:T(8,128)(2,1)}, bf16[512,128]{1,0:T(8,128)(2,1)}, bf16[128,512]{1,0:T(8,128)(2,1)}, bf16[128...) custom-call(bf16[512,128]{1,0:T(8,128)(2,1)} %get-tuple-element.12.refs_0_, bf16[512,128]{1,0:T(8,128)(2,1)} %get-tuple-element.13.refs_1_, ...), custom_call_target="tpu_custom_call" | custom-call | tf_op jit(solution)/shard_map/hand_over/pallas_call | solution.py:631

commit v3 on v2

--- a/solution.py
+++ b/solution.py
@@ -11,7 +11,8 @@
 BF = jnp.bfloat16
 F32 = jnp.float32
 MIB = 1 << 20
-N_SEM = 512
+N_SEND = 10
+N_RECV = 119
 
 
 def dot(a, b):
@@ -35,7 +36,7 @@
 
 
 def layer_kernel(
-    x, kk, a1, c1, c2, a2, wg, wu, wd, cot,
+    x_in, k_in, a1_in, c1_in, c2_in, a2_in, wg, wu, wd, cot_in,
     out, grad_in, grad_k, o_gate, o_up, o_down,
     wgf, wuf, wdf, feat, cotf,
     m1, m1t, m2, m2t, a1t, a2t,
@@ -44,7 +45,8 @@
     gg, gu, gd, coregot, turned, lhs_t,
     zr, swap_got, r1, r2, r3, r4, rhome, total,
     bmix, bspread, gks, binner, ihome, gkhome,
-    ssem, rsem,
+    x, kk, a1, c1, c2, a2, cot,
+    ssem, rsem, lsem,
 ):
     s = lax.axis_index("seq")
     t = lax.axis_index("tp")
@@ -70,50 +72,67 @@
             return plane(rem(y + (4 + d), 4), xx)
         return plane(y, rem(xx + (4 + d), 4))
 
-    count = [0]
-    sends = []
-
-    def remote(src, dst, dev):
-        i = count[0]
-        count[0] += 1
+    recv_bytes, send_bytes, late = [], [], []
+
+    def size(ref):
+        return 2 * math.prod(ref.shape)
+
+    def await_bytes(sem, n):
+        view = wgf.at[pl.ds(0, n // 1024), :]
+        pltpu.make_async_copy(view, view, sem).wait()
+
+    def group():
+        recv_bytes.append(0)
+        return len(recv_bytes) - 1
+
+    def wait(g):
+        await_bytes(rsem.at[g], recv_bytes[g])
+
+    def remote(src, dst, dev, g):
+        if not send_bytes or send_bytes[-1] + size(src) > 2 * MIB:
+            send_bytes.append(0)
+        send_bytes[-1] += size(src)
+        recv_bytes[g] += size(src)
         return pltpu.make_async_remote_copy(
-            src, dst, ssem.at[i], rsem.at[i], device_id=dev, device_id_type=MESH
+            src, dst, ssem.at[len(send_bytes) - 1], rsem.at[g],
+            device_id=dev, device_id_type=MESH,
         )
 
-    def send(src, dst, dev):
-        copy = remote(src, dst, dev)
-        copy.start()
-        sends.append(copy.wait_send)
-        return copy
+    def send(src, dst, dev, g):
+        remote(src, dst, dev, g).start()
+
+    def lone(src, dst, dev, k):
+        return pltpu.make_async_remote_copy(
+            src, dst, ssem.at[N_SEND + k], rsem.at[N_RECV + k],
+            device_id=dev, device_id_type=MESH,
+        )
 
     def exchange_order(i):
         k = div(i + 1, 2)
         return 8 + k * (2 * rem(i + 1, 2) - 1)
 
+    n_exchange = [0]
+
     def exchange(src, dst):
-        base = count[0]
-        count[0] += 15
-
-        def copy(i):
+        k = 8 + n_exchange[0]
+        n_exchange[0] += 1
+
+        def step(i, carry):
             j = rem(s + exchange_order(i), 16)
-            return pltpu.make_async_remote_copy(
+            pltpu.make_async_remote_copy(
                 src.at[pl.ds(mo(j * 32, 32), 32)],
                 dst.at[pl.ds(mo(s * 32, 32), 32)],
-                ssem.at[base + i], rsem.at[base + i],
+                ssem.at[N_SEND + k], rsem.at[N_RECV + k],
                 device_id=seq_dev(j), device_id_type=MESH,
-            )
-
-        def over(act):
-            def step(i, carry):
-                act(copy(i))
-                return carry
-            lax.fori_loop(0, 15, step, 0)
-
-        over(lambda p: p.start())
+            ).start()
+            return carry
+
+        lax.fori_loop(0, 15, step, 0)
         mine = pl.ds(mo(s * 32, 32), 32)
         dst[mine, :] = src[mine, :]
-        sends.append(lambda: over(lambda p: p.wait_send()))
-        return lambda: over(lambda p: p.wait_recv())
+        others = dst.at[pl.ds(0, 480), :]
+        late.append(lambda: pltpu.make_async_copy(others, others, ssem.at[N_SEND + k]).wait())
+        return lambda: pltpu.make_async_copy(others, others, rsem.at[N_RECV + k]).wait()
 
     def slot(ref, a, first, f, g, r0, nr):
         yy, xp = (f, g) if first == "y" else (g, f)
@@ -126,39 +145,42 @@
 
     def gather_plane(buf):
         halves = ((0, "y"), (1, "x"))
-        st1, st2 = {}, {}
+        both = ((0, 1), (1, -1))
+        st1, st2, fwd = {}, {}, {}
 
         def second(a, first, di):
             p1, p2, other = axes_of(first)
             f = rem(p1 + (4 + di), 4)
             piece = slot(buf, a, first, f, p2, 0, 128)
-            st2[a, di] = [send(piece, piece, nb(other, d)) for d in (1, -1)]
+            st2[a, di] = group()
+            for d in (1, -1):
+                send(piece, piece, nb(other, d), st2[a, di])
 
         def second_forward(a, first, di):
             p1, p2, other = axes_of(first)
             f = rem(p1 + (4 + di), 4)
-            got = []
-            for k, d in ((0, 1), (1, -1)):
-                st2[a, di][k].wait_recv()
+            wait(st2[a, di])
+            st2[a, di] = group()
+            for k, d in both:
                 piece = slot(buf, a, first, f, rem(p2 + (4 - d), 4), k * 64, 64)
-                got.append(send(piece, piece, nb(other, d)))
-            st2[a, di] = got
+                send(piece, piece, nb(other, d), st2[a, di])
 
         for a, first in halves:
             p1, p2, _ = axes_of(first)
             piece = slot(buf, a, first, p1, p2, 0, 128)
-            st1[a] = [send(piece, piece, nb(first, d)) for d in (1, -1)]
+            st1[a] = group()
+            for d in (1, -1):
+                send(piece, piece, nb(first, d), st1[a])
         for a, first in halves:
             second(a, first, 0)
         yield
-        fwd = {}
         for a, first in halves:
             p1, p2, _ = axes_of(first)
-            fwd[a] = []
-            for k, d in ((0, 1), (1, -1)):
-                st1[a][k].wait_recv()
+            fwd[a] = group()
+            wait(st1[a])
+            for k, d in both:
                 piece = slot(buf, a, first, rem(p1 + (4 - d), 4), p2, k * 64, 64)
-                fwd[a].append(send(piece, piece, nb(first, d)))
+                send(piece, piece, nb(first, d), fwd[a])
         for a, first in halves:
             second(a, first, -1)
             second(a, first, 1)
@@ -167,8 +189,7 @@
             second_forward(a, first, 0)
         yield
         for a, first in halves:
-            for copy in fwd[a]:
-                copy.wait_recv()
+            wait(fwd[a])
             second(a, first, 2)
         yield
         for di in (-1, 1):
@@ -180,8 +201,7 @@
         yield
         for di in (0, -1, 1, 2):
             for a, first in halves:
-                for copy in st2[a, di]:
-                    copy.wait_recv()
+                wait(st2[a, di])
 
     def add_into(ref, *others):
         value = ref[...].astype(F32)
@@ -191,72 +211,63 @@
 
     def scatter_plane(buf, w):
         halves = ((0, "x"), (1, "y"))
+        both = ((0, 1), (1, -1))
         order = (2, 1, -1, 0)
         st1, st2, st3, st4 = {}, {}, {}, {}
         for gi, dg in enumerate(order):
             for a, first in halves:
                 p1, p2, _ = axes_of(first)
                 f, g = rem(p1 + 2, 4), rem(p2 + (4 + dg), 4)
-                st1[a, gi] = [
-                    send(
-                        slot(buf, a, first, f, g, k * 64, 64), r1.at[w, a, gi, k], nb(first, d)
-                    )
-                    for k, d in ((0, 1), (1, -1))
-                ]
+                st1[a, gi] = group()
+                for k, d in both:
+                    piece = slot(buf, a, first, f, g, k * 64, 64)
+                    send(piece, r1.at[w, a, gi, k], nb(first, d), st1[a, gi])
         yield
         for gi, dg in enumerate(order):
             for a, first in halves:
                 p1, p2, _ = axes_of(first)
                 g = rem(p2 + (4 + dg), 4)
-                st2[a, gi] = []
-                for k, d in ((0, 1), (1, -1)):
-                    st1[a, gi][k].wait_recv()
+                st2[a, gi] = group()
+                wait(st1[a, gi])
+                for k, d in both:
                     f = rem(p1 + (4 + d), 4)
                     add_into(slot(buf, a, first, f, g, k * 64, 64), r1.at[w, a, gi, k])
-                    st2[a, gi].append(
-                        send(
-                            slot(buf, a, first, f, g, 0, 128), r2.at[w, a, gi, k], nb(first, d)
-                        )
-                    )
+                    piece = slot(buf, a, first, f, g, 0, 128)
+                    send(piece, r2.at[w, a, gi, k], nb(first, d), st2[a, gi])
             yield
         for gi, dg in enumerate(order):
             for a, first in halves:
                 p1, p2, other = axes_of(first)
                 g = rem(p2 + (4 + dg), 4)
-                for copy in st2[a, gi]:
-                    copy.wait_recv()
+                wait(st2[a, gi])
                 add_into(
                     slot(buf, a, first, p1, g, 0, 128), r2.at[w, a, gi, 0], r2.at[w, a, gi, 1]
                 )
                 if dg == 2:
-                    st3[a] = [
-                        send(
-                            slot(buf, a, first, p1, g, k * 64, 64), r3.at[w, a, k], nb(other, d)
-                        )
-                        for k, d in ((0, 1), (1, -1))
-                    ]
+                    st3[a] = group()
+                    for k, d in both:
+                        piece = slot(buf, a, first, p1, g, k * 64, 64)
+                        send(piece, r3.at[w, a, k], nb(other, d), st3[a])
             yield
         for a, first in halves:
             p1, p2, other = axes_of(first)
-            st4[a] = []
-            for k, d in ((0, 1), (1, -1)):
+            st4[a] = group()
+            wait(st3[a])
+            for k, d in both:
                 g = rem(p2 + (4 + d), 4)
-                st3[a][k].wait_recv()
                 add_into(slot(buf, a, first, p1, g, k * 64, 64), r3.at[w, a, k])
-                st4[a].append(
-                    send(slot(buf, a, first, p1, g, 0, 128), r4.at[w, a, k], nb(other, d))
-                )
+                send(slot(buf, a, first, p1, g, 0, 128), r4.at[w, a, k], nb(other, d), st4[a])
         yield
         for a, first in halves:
             p1, p2, other = axes_of(first)
-            for copy in st4[a]:
-                copy.wait_recv()
+            wait(st4[a])
             add_into(slot(buf, a, first, p1, p2, 0, 128), r4.at[w, a, 0], r4.at[w, a, 1])
         rows = pl.ds(mo(h * 256, 256), 256)
         cols = pl.ds(mo((y * 2 + l) * 256 + (1 - c) * 128, 128), 128)
-        back = send(buf.at[rows, cols], rhome.at[w], core_dev)
-        yield
-        back.wait_recv()
+        back = group()
+        send(buf.at[rows, cols], rhome.at[w], core_dev, back)
+        yield
+        wait(back)
 
     half_rows = pl.ds(mo(c * 256, 256), 256)
     other_rows = pl.ds(mo((1 - c) * 256, 256), 256)
@@ -264,9 +275,10 @@
     my_cols = pl.ds(mo((y * 2 + l) * 256 + c * 128, 128), 128)
 
     def share_core(src, buf):
-        copy = send(src.at[other_rows], buf.at[my_rows, my_cols], core_dev)
+        g = group()
+        send(src.at[other_rows], buf.at[my_rows, my_cols], core_dev, g)
         buf[my_rows, my_cols] = src[half_rows, :]
-        return copy
+        return g
 
     def wslice(w, j, part=None):
         ref = (wdf, wgf, wuf)[w]
@@ -278,20 +290,16 @@
         return ref.at[pl.ds(mo(j * 128 + part * 64, 64), 64), :]
 
     wsrc = (wd, wg, wu)
-    core_waits = []
-
     def ring_weights():
-        swaps = [remote(wsrc[w], wslice(w, s), swap_dev) for w in range(3)]
-        pend = {}
-        first = {}
+        swaps = [lone(wsrc[w], wslice(w, s), swap_dev, w) for w in range(3)]
+        own = [pltpu.make_async_copy(wsrc[w], wslice(w, s), lsem.at[7 + w]) for w in range(3)]
+        cores = [group() for w in range(3)]
+        pend = [group() for w in range(3)]
+        first = []
         for w in range(3):
             piece = wslice(w, z * 2 + c)
-            pend[w, 1] = remote(piece, piece, z_dev(1))
-            pend[w, -1] = remote(piece, piece, z_dev(-1))
-            first[w] = [pend[w, 1], pend[w, -1], remote(piece, piece, core_dev)]
-            for copy in first[w]:
-                sends.append(copy.wait_send)
-            core_waits.append(first[w][2])
+            first.append([remote(piece, piece, z_dev(d), pend[w]) for d in (1, -1)])
+            first[w].append(remote(piece, piece, core_dev, cores[w]))
 
         @pl.when(jnp.logical_not(own_side))
         def _():
@@ -300,8 +308,10 @@
 
         @pl.when(own_side)
         def _():
+            for copy in own:
+                copy.start()
             for w in range(3):
-                wslice(w, s)[...] = wsrc[w][...]
+                own[w].wait()
                 for copy in first[w]:
                     copy.start()
 
@@ -311,16 +321,12 @@
                 for copy in swaps:
                     copy.wait_send()
 
-        sends.append(wait_swaps)
-        yield
-
-        def pass_on(w, dz, d, part=None):
-            piece = wslice(w, rem(z + (8 + dz), 8) * 2 + c, part)
-            pend[w, d] = send(piece, piece, z_dev(d))
+        late.append(wait_swaps)
+        yield
 
         def to_core(w, dz):
             piece = wslice(w, rem(z + (8 + dz), 8) * 2 + c)
-            core_waits.append(send(piece, piece, core_dev))
+            send(piece, piece, core_dev, cores[w])
 
         @pl.when(jnp.logical_not(own_side))
         def _():
@@ -332,20 +338,21 @@
         yield
         for k in (1, 2, 3):
             for w in range(3):
+                wait(pend[w])
+                pend[w] = group()
                 for d in (1, -1):
-                    pend[w, d].wait_recv()
                     part = None if k < 3 else (0 if d == 1 else 1)
-                    pass_on(w, -d * k, d, part)
+                    piece = wslice(w, rem(z + (8 - d * k), 8) * 2 + c, part)
+                    send(piece, piece, z_dev(d), pend[w])
                 for d in (1, -1):
                     to_core(w, -d * k)
                 yield
         for w in range(3):
-            for d in (1, -1):
-                pend[w, d].wait_recv()
+            wait(pend[w])
             to_core(w, 4)
         yield
-        for copy in core_waits:
-            copy.wait_recv()
+        for w in range(3):
+            wait(cores[w])
 
     gbufs = (gg, gu, gd)
     got_core = {}
@@ -355,9 +362,10 @@
         zz = rem(z + (8 + zorder[i]), 8)
         cols = pl.ds(mo(zz * 256, 256), 256)
         there = pl.ds(mo(zz * 256 + (1 - c) * 128, 128), 128)
+        got_core[i] = group()
         for w, rhs in ((0, feat), (1, feat), (2, cotf)):
             gbufs[w][:, cols] = (dot(lhs_t[w], rhs[:, cols]) * scale).astype(BF)
-            got_core[w, i] = send(gbufs[w].at[:, there], coregot.at[w, i], core_dev)
+            send(gbufs[w].at[:, there], coregot.at[w, i], core_dev, got_core[i])
 
     def mine_block(w, dz, part=None):
         zz = rem(z + (8 + dz), 8)
@@ -366,51 +374,44 @@
         return gbufs[w].at[rows, cols]
 
     def core_sum(i):
+        wait(got_core[i])
         for w in range(3):
-            got_core[w, i].wait_recv()
             add_into(mine_block(w, zorder[i]), coregot.at[w, i])
 
     def ring_grads():
         pend = {}
+        wait(got_core[0])
         for w in range(3):
-            got_core[w, 0].wait_recv()
             add_into(mine_block(w, 4), coregot.at[w, 0])
-            pend[w] = [
-                send(mine_block(w, 4, k), zr.at[w, 0, k, pl.ds(0, 256)], z_dev(d))
-                for k, d in ((0, 1), (1, -1))
-            ]
+            pend[w] = group()
+            for k, d in ((0, 1), (1, -1)):
+                send(mine_block(w, 4, k), zr.at[w, 0, k, pl.ds(0, 256)], z_dev(d), pend[w])
         yield
         for n in (3, 2, 1):
             for w in range(3):
-                new = []
+                wait(pend[w])
+                pend[w] = group()
                 for k, d in ((0, 1), (1, -1)):
-                    pend[w][k].wait_recv()
                     if n == 3:
                         add_into(mine_block(w, d * n, k), zr.at[w, 0, k, pl.ds(0, 256)])
                     else:
                         add_into(mine_block(w, d * n), zr.at[w, 3 - n, k])
-                    new.append(send(mine_block(w, d * n), zr.at[w, 4 - n, k], z_dev(d)))
-                pend[w] = new
+                    send(mine_block(w, d * n), zr.at[w, 4 - n, k], z_dev(d), pend[w])
                 yield
-        swaps = []
+        swaps = [lone(mine_block(w, 0), swap_got.at[w], swap_dev, 3 + w) for w in range(3)]
         for w in range(3):
-            for copy in pend[w]:
-                copy.wait_recv()
+            wait(pend[w])
             add_into(mine_block(w, 0), zr.at[w, 3, 0], zr.at[w, 3, 1])
-            swap = remote(mine_block(w, 0), swap_got.at[w], swap_dev)
-            swaps.append(swap)
 
             @pl.when(jnp.logical_not(own_side))
             def _():
-                swap.start()
+                swaps[w].start()
 
             yield
         for w in range(3):
-            swap = swaps[w]
-
             @pl.when(jnp.logical_not(own_side))
             def _():
-                swap.wait()
+                swaps[w].wait()
 
             @pl.when(own_side)
             def _():
@@ -433,11 +434,24 @@
             pass
 
     scale = 1.0 / math.sqrt(8192.0)
+    fetch = [
+        pltpu.make_async_copy(src, dst, lsem.at[i])
+        for i, (src, dst) in enumerate(
+            (
+                (x_in, x), (a1_in, a1), (c1_in, c1), (cot_in, cot), (k_in, kk),
+                (c2_in, c2), (a2_in, a2),
+            )
+        )
+    ]
+    for copy in fetch:
+        copy.start()
     barrier = pltpu.get_barrier_semaphore()
     partners = [seq_dev(rem(s + d, 16)) for d in range(1, 16)]
     partners += [nb("y", 1), nb("y", -1), nb("x", 1), nb("x", -1), core_dev, swap_dev]
     for dev in partners:
         pl.semaphore_signal(barrier, inc=1, device_id=dev, device_id_type=MESH)
+    fetch[0].wait()
+    fetch[1].wait()
     inner[...] = dot(a1[...], x[...]).astype(BF)
 
     row = lax.broadcasted_iota(jnp.int32, (256, 512), 0)
@@ -455,7 +469,10 @@
             turned[pl.ds(i * 32, 32), :] = moved.astype(BF)
         m[...] = jnp.where(diag, dot(turned[...], picked), 0.0).astype(BF)
 
+    fetch[2].wait()
     widen(c1, m1, 16, pick)
+    for copy in fetch[3:]:
+        copy.wait()
     pl.semaphore_wait(barrier, len(partners))
 
     got_inner = exchange(inner, spread)
@@ -464,7 +481,7 @@
     got_cot = share_core(cot, cotf)
     got_k = exchange(kk, kspread)
     widen(c2, m2, 16, pick)
-    got_cot.wait_recv()
+    wait(got_cot)
     cot_flow = gather_plane(cotf)
     run(cot_flow)
     run(weights)
@@ -486,7 +503,7 @@
     hid_in[...] = (x[...].astype(F32) + dot(a2[...], mhome[...])).astype(BF)
     got_feat = share_core(hid_in, feat)
     run(weights)
-    got_feat.wait_recv()
+    wait(got_feat)
     feat_flow = gather_plane(feat)
     run(feat_flow)
     run(cot_flow)
@@ -585,9 +602,12 @@
     ).astype(BF)
     out[other_rows, :] = (hid_in[other_rows, :].astype(F32) + rhome[1].astype(F32)).astype(BF)
     drain(grads)
-    for wait in sends:
-        wait()
-    assert count[0] <= N_SEM, count[0]
+    for finish in late:
+        finish()
+    for i, n in enumerate(send_bytes):
+        await_bytes(ssem.at[i], n)
+    assert len(send_bytes) == N_SEND, len(send_bytes)
+    assert len(recv_bytes) == N_RECV, len(recv_bytes)
 
 
 def hand_over(*refs):
@@ -614,14 +634,21 @@
         vm((2, 256, 128), BF), vm((512, 128), F32),
     ]
     scratch += [vm((512, 128), BF)] * 6
-    scratch += [pltpu.SemaphoreType.DMA((N_SEM,)), pltpu.SemaphoreType.DMA((N_SEM,))]
+    scratch += [
+        vm((512, 128), BF), vm((512, 128), BF), vm((512, 512), BF), vm((32, 256), BF),
+        vm((32, 256), BF), vm((512, 512), BF), vm((512, 128), BF),
+    ]
+    scratch += [
+        pltpu.SemaphoreType.DMA((N_SEND + 14,)), pltpu.SemaphoreType.DMA((N_RECV + 14,)),
+        pltpu.SemaphoreType.DMA((10,)),
+    ]
     wide = jax.ShapeDtypeStruct((512, 128), BF)
     tall = jax.ShapeDtypeStruct((128, 512), BF)
     results = pl.pallas_call(
         layer_kernel,
         name="mixer_layer",
         out_shape=[wide, wide, wide, tall, tall, wide],
-        in_specs=[pl.BlockSpec(memory_space=vm)] * 10,
+        in_specs=[pl.BlockSpec(memory_space=pl.ANY)] * 10,
         out_specs=[pl.BlockSpec(memory_space=vm)] * 6,
         scratch_shapes=scratch,
         compiler_params=pltpu.CompilerParams(

time: 127 us -> 117 us (0.921)
  Pallas kernels: 125 us -> 116 us
    pallas_call x1, Pallas kernels: 123 us -> 114 us  [per_device(): pl.pallas_call(layer_kernel, name='mixer_layer', out_shape=[wide, wide, w...]
where the time goes in v3:
time: 117 us
  Pallas kernels  116 us (99%)
    pallas_call x1, Pallas kernels, per_device(): pl.pallas_call(layer_kernel, name='mixer_layer', out_shape=[wide, wide, w...  114 us

profile of v3, /device:TPU:1, one launch (start us, length us, event | category | flops | bytes accessed | tf_op | source)
XLA Modules:
  0.0 117.1 jit_solution(11990369270073165747)
XLA Ops:
  0.6 114.4 %mixer_layer.1 = (bf16[512,128]{1,0:T(8,128)(2,1)}, bf16[512,128]{1,0:T(8,128)(2,1)}, bf16[512,128]{1,0:T(8,128)(2,1)}, bf16[128,512]{1,0:T(8,128)(2,1)}, bf16[1...) custom-call(bf16[512,128]{1,0:T(8,128)(2,1)} %x_in.1, bf16[512,128]{1,0:T(8,128)(2,1)} %k_in.1, bf16[512,512]{1,0:T(8,128)(2,1)} %a1_in.1, ...), custom_call_target="tpu_custom_call" | custom-call | tf_op jit(solution)/shard_map/mixer_layer/pallas_call | solution.py:647
  115.0 2.1 %hand_over.1 = (bf16[512,128]{1,0:T(8,128)(2,1)}, bf16[512,128]{1,0:T(8,128)(2,1)}, bf16[512,128]{1,0:T(8,128)(2,1)}, bf16[128,512]{1,0:T(8,128)(2,1)}, bf16[128...) custom-call(bf16[512,128]{1,0:T(8,128)(2,1)} %get-tuple-element.12.refs_0_, bf16[512,128]{1,0:T(8,128)(2,1)} %get-tuple-element.13.refs_1_, ...), custom_call_target="tpu_custom_call" | custom-call | tf_op jit(solution)/shard_map/hand_over/pallas_call | solution.py:658

commit v4 on v3

--- a/solution.py
+++ b/solution.py
@@ -11,7 +11,9 @@
 BF = jnp.bfloat16
 F32 = jnp.float32
 MIB = 1 << 20
-N_SEND = 10
+FIRST = ("x1 w0 sc xk", "m2 c0 W t1", "cb C W W", "W t2 C mt", "C hm W f0", "C W W F", "C W F -C", "W F W F", "F W W bh", "W -F W gt", "W")
+SECOND = ("ga g1 G bp", "B s1 g2 G", "B G B G", "B B s2 B", "B G B B", "G dp B G", "x3 D G D", "D D D G", "cx G D D", "D D D G", "D fi G fk", "fo -G")
+N_SEND = 9
 N_RECV = 119
 
 
@@ -38,16 +40,17 @@
 def layer_kernel(
     x_in, k_in, a1_in, c1_in, c2_in, a2_in, wg, wu, wd, cot_in,
     out, grad_in, grad_k, o_gate, o_up, o_down,
-    wgf, wuf, wdf, feat, cotf,
+    wgf, wuf, wdf, acts,
     m1, m1t, m2, m2t, a1t, a2t,
     inner, spread, kspread, crossed, mixed, mhome, hid_in,
-    bh, hidden, bgate, bup, bt, dt,
-    gg, gu, gd, coregot, turned, lhs_t,
+    bh, gates, hidden, bgate, bup, bt, dt,
+    gall, coregot, turned, lhs_t,
     zr, swap_got, r1, r2, r3, r4, rhome, total,
     bmix, bspread, gks, binner, ihome, gkhome,
     x, kk, a1, c1, c2, a2, cot,
     ssem, rsem, lsem,
 ):
+    feat, cotf = acts.at[0], acts.at[1]
     s = lax.axis_index("seq")
     t = lax.axis_index("tp")
     z, h = div(s, 2), rem(s, 2)
@@ -107,27 +110,20 @@
             device_id=dev, device_id_type=MESH,
         )
 
-    def exchange_order(i):
-        k = div(i + 1, 2)
-        return 8 + k * (2 * rem(i + 1, 2) - 1)
-
     n_exchange = [0]
 
     def exchange(src, dst):
         k = 8 + n_exchange[0]
         n_exchange[0] += 1
 
-        def step(i, carry):
-            j = rem(s + exchange_order(i), 16)
+        for d in (8, 7, 9, 6, 10, 5, 11, 4, 12, 3, 13, 2, 14, 1, 15):
+            j = rem(s + d, 16)
             pltpu.make_async_remote_copy(
                 src.at[pl.ds(mo(j * 32, 32), 32)],
                 dst.at[pl.ds(mo(s * 32, 32), 32)],
                 ssem.at[N_SEND + k], rsem.at[N_RECV + k],
                 device_id=seq_dev(j), device_id_type=MESH,
             ).start()
-            return carry
-
-        lax.fori_loop(0, 15, step, 0)
         mine = pl.ds(mo(s * 32, 32), 32)
         dst[mine, :] = src[mine, :]
         others = dst.at[pl.ds(0, 480), :]
@@ -347,42 +343,61 @@
                 for d in (1, -1):
                     to_core(w, -d * k)
                 yield
-        for w in range(3):
+        for w in (0, 1):
             wait(pend[w])
             to_core(w, 4)
         yield
-        for w in range(3):
-            wait(cores[w])
-
-    gbufs = (gg, gu, gd)
-    got_core = {}
-    zorder = (4, 3, -3, 2, -2, 1, -1, 0)
-
-    def grad_tiles(i):
-        zz = rem(z + (8 + zorder[i]), 8)
-        cols = pl.ds(mo(zz * 256, 256), 256)
-        there = pl.ds(mo(zz * 256 + (1 - c) * 128, 128), 128)
-        got_core[i] = group()
-        for w, rhs in ((0, feat), (1, feat), (2, cotf)):
-            gbufs[w][:, cols] = (dot(lhs_t[w], rhs[:, cols]) * scale).astype(BF)
-            send(gbufs[w].at[:, there], coregot.at[w, i], core_dev, got_core[i])
+        wait(cores[0])
+        yield
+        wait(pend[2])
+        to_core(2, 4)
+        yield
+        wait(cores[1])
+        yield
+        wait(cores[2])
+        yield
+
+    tile_sem = []
+
+    def ring_place(i):
+        return rem(z + (8 + (4, 3, -3, 2, -2, 1, -1, 0)[i]), 8)
+
+    def grad_tiles(lo, hi):
+        if not tile_sem:
+            tile_sem.append(len(recv_bytes))
+            recv_bytes.extend([3 * 512 * 128 * 2] * 8)
+            for i in range(8):
+                late.append(lambda i=i: await_bytes(ssem.at[N_SEND + 14 + i], 3 * 512 * 128 * 2))
+
+        for i in range(lo, hi):
+            zz = ring_place(i)
+            cols = pl.ds(mo(zz * 256, 256), 256)
+            there = pl.ds(mo(zz * 256 + (1 - c) * 128, 128), 128)
+            for w in range(3):
+                gall[w, :, cols] = (dot(lhs_t[w], acts[w // 2, :, cols]) * scale).astype(BF)
+                pltpu.make_async_remote_copy(
+                    gall.at[w, :, there], coregot.at[w, i],
+                    ssem.at[N_SEND + 14 + i], rsem.at[tile_sem[0] + i],
+                    device_id=core_dev, device_id_type=MESH,
+                ).start()
 
     def mine_block(w, dz, part=None):
         zz = rem(z + (8 + dz), 8)
         cols = pl.ds(mo(zz * 256 + c * 128, 128), 128)
         rows = pl.ds(0, 512) if part is None else pl.ds(part * 256, 256)
-        return gbufs[w].at[rows, cols]
-
-    def core_sum(i):
-        wait(got_core[i])
-        for w in range(3):
-            add_into(mine_block(w, zorder[i]), coregot.at[w, i])
+        return gall.at[w, rows, cols]
+
+    def core_sum(lo, hi):
+        for i in range(lo, hi):
+            await_bytes(rsem.at[tile_sem[0] + i], 3 * 512 * 128 * 2)
+            cols = pl.ds(mo(ring_place(i) * 256 + c * 128, 128), 128)
+            for w in range(3):
+                add_into(gall.at[w, :, cols], coregot.at[w, i])
 
     def ring_grads():
         pend = {}
-        wait(got_core[0])
+        core_sum(0, 1)
         for w in range(3):
-            add_into(mine_block(w, 4), coregot.at[w, 0])
             pend[w] = group()
             for k, d in ((0, 1), (1, -1)):
                 send(mine_block(w, 4, k), zr.at[w, 0, k, pl.ds(0, 256)], z_dev(d), pend[w])
@@ -475,133 +490,154 @@
         copy.wait()
     pl.semaphore_wait(barrier, len(partners))
 
-    got_inner = exchange(inner, spread)
-    weights = ring_weights()
-    run(weights)
-    got_cot = share_core(cot, cotf)
-    got_k = exchange(kk, kspread)
-    widen(c2, m2, 16, pick)
-    wait(got_cot)
-    cot_flow = gather_plane(cotf)
-    run(cot_flow)
-    run(weights)
-    a1t[...] = a1[...].T
-    got_inner()
-    crossed[...] = dot(m1[...], spread[...]).astype(BF)
-    got_k()
-    scaled = (kspread[...].astype(F32) * crossed[...].astype(F32)).astype(BF)
-    mixed[...] = dot(m2[...], scaled).astype(BF)
-    got_mixed = exchange(mixed, mhome)
-    run(cot_flow)
-    run(weights, 3)
-    a2t[...] = a2[...].T
-    run(cot_flow)
-    widen(c1, m1t, 1, pick_t)
-    widen(c2, m2t, 1, pick_t)
-    run(cot_flow)
-    got_mixed()
-    hid_in[...] = (x[...].astype(F32) + dot(a2[...], mhome[...])).astype(BF)
-    got_feat = share_core(hid_in, feat)
-    run(weights)
-    wait(got_feat)
-    feat_flow = gather_plane(feat)
-    run(feat_flow)
-    run(cot_flow)
-    run(weights, 2)
-    run(feat_flow)
-    run(cot_flow)
-    run(weights, 1)
-    run(feat_flow)
-    drain(cot_flow)
-    run(weights, 1)
-    run(feat_flow)
-    run(weights, 1)
-    run(feat_flow)
-    run(feat_flow)
-    drain(weights)
-    for j in range(2):
-        cols = pl.ds(j * 256, 256)
-        bh[:, cols] = dot_nt(cotf[...], wdf[cols, :])
-    drain(feat_flow)
-
-    for j in range(2):
-        cols = pl.ds(j * 256, 256)
-        gate = dot(feat[...], wgf[:, cols])
-        up = dot(feat[...], wuf[:, cols])
-        sig = 1.0 / (1.0 + jnp.exp(-gate))
-        back = bh[:, cols]
-        hid = (gate * sig * up).astype(BF)
-        hidden[:, cols] = hid
-        lhs_t[2, cols, :] = hid.T
-        bg = (back * up * sig * (1.0 + gate * (1.0 - sig))).astype(BF)
-        bgate[:, cols] = bg
-        lhs_t[0, cols, :] = bg.T
-        bu = (back * gate * sig).astype(BF)
-        bup[:, cols] = bu
-        lhs_t[1, cols, :] = bu.T
-    grad_tiles(0)
-    grad_tiles(1)
-    grad_tiles(2)
-    grads = ring_grads()
-    run(grads)
-    for j in range(8):
-        rows = pl.ds(j * 256, 256)
-        bt[:, rows] = (dot_nt(bgate[...], wgf[rows, :]) + dot_nt(bup[...], wuf[rows, :])).astype(BF)
-    back_flow = scatter_plane(bt, 0)
-    run(back_flow)
-    core_sum(1)
-    core_sum(2)
-    for i in range(3, 8):
-        grad_tiles(i)
-    run(grads)
-    run(back_flow)
-    run(grads)
-    run(back_flow)
-    run(grads)
-    run(back_flow, 2)
-    for i in range(3, 8):
-        core_sum(i)
-    run(back_flow, 2)
-    run(grads)
-    run(back_flow, 2)
-    run(grads)
-    for j in range(8):
-        cols = pl.ds(j * 256, 256)
-        dt[:, cols] = dot(hidden[...], wdf[:, cols]).astype(BF)
-    run(back_flow)
-    run(grads)
-    drain(back_flow)
-    total[half_rows, :] = cot[half_rows, :].astype(F32) + bt[my_rows, my_cols].astype(F32)
-    total[other_rows, :] = cot[other_rows, :].astype(F32) + rhome[0].astype(F32)
-    bmix[...] = dot(a2t[...], total[...].astype(BF)).astype(BF)
-    got_back = exchange(bmix, bspread)
-    down_flow = scatter_plane(dt, 1)
-    run(down_flow)
-    run(grads)
-    run(down_flow, 4)
-    run(grads)
-    got_back()
-    bscaled = dot(m2t[...], bspread[...]).astype(BF).astype(F32)
-    bcrossed = (bscaled * kspread[...].astype(F32)).astype(BF)
-    binner[...] = dot(m1t[...], bcrossed).astype(BF)
-    got_binner = exchange(binner, ihome)
-    gks[...] = (bscaled * crossed[...].astype(F32)).astype(BF)
-    got_gk = exchange(gks, gkhome)
-    run(grads)
-    run(down_flow, 5)
-    run(grads)
-    run(down_flow)
-    got_binner()
-    grad_in[...] = (total[...] + dot(a1t[...], ihome[...])).astype(BF)
-    run(grads)
-    got_gk()
-    grad_k[...] = gkhome[...]
-    drain(down_flow)
-    out[half_rows, :] = (
-        hid_in[half_rows, :].astype(F32) + dt[my_rows, my_cols].astype(F32)
-    ).astype(BF)
-    out[other_rows, :] = (hid_in[other_rows, :].astype(F32) + rhome[1].astype(F32)).astype(BF)
-    drain(grads)
+    flows = {}
+    got = {}
+
+    def start_mix():
+        got["inner"] = exchange(inner, spread)
+
+    def start_weights():
+        flows["W"] = ring_weights()
+        run(flows["W"])
+
+    def share_cot():
+        got["cot"] = share_core(cot, cotf)
+
+    def start_k():
+        got["k"] = exchange(kk, kspread)
+
+    def widen_second():
+        widen(c2, m2, 16, pick)
+
+    def start_cot():
+        wait(got["cot"])
+        flows["C"] = gather_plane(cotf)
+        run(flows["C"])
+
+    def turn_first():
+        a1t[...] = a1[...].T
+
+    def turn_second():
+        a2t[...] = a2[...].T
+
+    def cross_blocks():
+        got["inner"]()
+        crossed[...] = dot(m1[...], spread[...]).astype(BF)
+        got["k"]()
+        scaled = (kspread[...].astype(F32) * crossed[...].astype(F32)).astype(BF)
+        mixed[...] = dot(m2[...], scaled).astype(BF)
+        got["mixed"] = exchange(mixed, mhome)
+
+    def widen_turned():
+        widen(c1, m1t, 1, pick_t)
+        widen(c2, m2t, 1, pick_t)
+
+    def home():
+        got["mixed"]()
+        hid_in[...] = (x[...].astype(F32) + dot(a2[...], mhome[...])).astype(BF)
+        got["feat"] = share_core(hid_in, feat)
+
+    def start_feat():
+        wait(got["feat"])
+        flows["F"] = gather_plane(feat)
+        run(flows["F"])
+
+    def back_hidden():
+        for j in range(2):
+            cols = pl.ds(mo(j * 256, 256), 256)
+            bh[:, cols] = dot_nt(cotf[...], wdf[cols, :])
+
+    def gate_product():
+        for j in range(2):
+            cols = pl.ds(mo(j * 256, 256), 256)
+            gates[:, cols] = dot(feat[...], wgf[:, cols])
+
+    def gated():
+        for j in range(2):
+            cols = pl.ds(mo(j * 256, 256), 256)
+            gate = gates[:, cols]
+            up = dot(feat[...], wuf[:, cols])
+            sig = 1.0 / (1.0 + jnp.exp(-gate))
+            back = bh[:, cols]
+            hid = (gate * sig * up).astype(BF)
+            hidden[:, cols] = hid
+            lhs_t[2, cols, :] = hid.T
+            bg = (back * up * sig * (1.0 + gate * (1.0 - sig))).astype(BF)
+            bgate[:, cols] = bg
+            lhs_t[0, cols, :] = bg.T
+            bu = (back * gate * sig).astype(BF)
+            bup[:, cols] = bu
+            lhs_t[1, cols, :] = bu.T
+
+        flows["G"] = ring_grads()
+
+    def back_product():
+        for j in range(8):
+            rows = pl.ds(mo(j * 256, 256), 256)
+            bt[:, rows] = (
+                dot_nt(bgate[...], wgf[rows, :]) + dot_nt(bup[...], wuf[rows, :])
+            ).astype(BF)
+
+        flows["B"] = scatter_plane(bt, 0)
+
+    def down_product():
+        for j in range(8):
+            cols = pl.ds(mo(j * 256, 256), 256)
+            dt[:, cols] = dot(hidden[...], wdf[:, cols]).astype(BF)
+
+        flows["D"] = scatter_plane(dt, 1)
+
+    def back_home():
+        drain(flows["B"])
+        total[half_rows, :] = cot[half_rows, :].astype(F32) + bt[my_rows, my_cols].astype(F32)
+        total[other_rows, :] = cot[other_rows, :].astype(F32) + rhome[0].astype(F32)
+        bmix[...] = dot(a2t[...], total[...].astype(BF)).astype(BF)
+        got["back"] = exchange(bmix, bspread)
+
+    def cross_back():
+        got["back"]()
+        bscaled = dot(m2t[...], bspread[...]).astype(BF).astype(F32)
+        bcrossed = (bscaled * kspread[...].astype(F32)).astype(BF)
+        binner[...] = dot(m1t[...], bcrossed).astype(BF)
+        got["binner"] = exchange(binner, ihome)
+        gks[...] = (bscaled * crossed[...].astype(F32)).astype(BF)
+        got["gk"] = exchange(gks, gkhome)
+
+    def finish_inputs():
+        got["binner"]()
+        grad_in[...] = (total[...] + dot(a1t[...], ihome[...])).astype(BF)
+
+    def finish_kernel():
+        got["gk"]()
+        grad_k[...] = gkhome[...]
+
+    def finish_output():
+        drain(flows["D"])
+        out[half_rows, :] = (
+            hid_in[half_rows, :].astype(F32) + dt[my_rows, my_cols].astype(F32)
+        ).astype(BF)
+        out[other_rows, :] = (
+            hid_in[other_rows, :].astype(F32) + rhome[1].astype(F32)
+        ).astype(BF)
+
+    steps = {
+        "x1": start_mix, "w0": start_weights, "sc": share_cot, "xk": start_k,
+        "m2": widen_second, "c0": start_cot, "t1": turn_first, "t2": turn_second,
+        "cb": cross_blocks, "mt": widen_turned, "hm": home, "f0": start_feat,
+        "bh": back_hidden, "ga": gated, "gt": gate_product, "bp": back_product, "dp": down_product,
+        "x3": back_home, "cx": cross_back, "fi": finish_inputs, "fk": finish_kernel,
+        "fo": finish_output,
+        "g1": lambda: grad_tiles(0, 3), "g2": lambda: grad_tiles(3, 8),
+        "s1": lambda: core_sum(1, 3), "s2": lambda: core_sum(3, 8),
+    }
+    for line in FIRST + SECOND:
+        for name in line.split():
+            if name in steps:
+                steps[name]()
+            elif name[0] == "-":
+                drain(flows[name[1]])
+            else:
+                run(flows[name])
     for finish in late:
         finish()
     for i, n in enumerate(send_bytes):
@@ -619,13 +655,13 @@
     vm = pltpu.VMEM
     scratch = [
         vm((2048, 512), BF), vm((2048, 512), BF), vm((512, 2048), BF),
-        vm((512, 2048), BF), vm((512, 2048), BF),
+        vm((2, 512, 2048), BF),
     ]
     scratch += [vm((512, 512), BF)] * 6
     scratch += [vm((512, 128), BF)] * 7
-    scratch += [vm((512, 512), F32)] + [vm((512, 512), BF)] * 3
+    scratch += [vm((512, 512), F32)] * 2 + [vm((512, 512), BF)] * 3
     scratch += [vm((512, 2048), BF)] * 2
-    scratch += [vm((512, 2048), BF)] * 3
+    scratch += [vm((3, 512, 2048), BF)]
     scratch += [vm((3, 8, 512, 128), BF), vm((512, 256), BF), vm((3, 512, 512), BF)]
     scratch += [
         vm((3, 4, 2, 512, 128), BF), vm((3, 512, 128), BF),
@@ -639,7 +675,7 @@
         vm((32, 256), BF), vm((512, 512), BF), vm((512, 128), BF),
     ]
     scratch += [
-        pltpu.SemaphoreType.DMA((N_SEND + 14,)), pltpu.SemaphoreType.DMA((N_RECV + 14,)),
+        pltpu.SemaphoreType.DMA((N_SEND + 22,)), pltpu.SemaphoreType.DMA((N_RECV + 14,)),
         pltpu.SemaphoreType.DMA((10,)),
     ]
     wide = jax.ShapeDtypeStruct((512, 128), BF)

time: 117 us -> 117 us (level)
  no operation moved by 1% of the time
where the time goes in v4:
time: 117 us
  Pallas kernels  116 us (99%)
    pallas_call x1, Pallas kernels, per_device(): pl.pallas_call(layer_kernel, name='mixer_layer', out_shape=[wide, wide, w...  114 us

profile of v4, /device:TPU:1, one launch (start us, length us, event | category | flops | bytes accessed | tf_op | source)
XLA Modules:
  0.0 116.6 jit_solution(2784360059888612807)
XLA Ops:
  0.6 113.8 %mixer_layer.1 = (bf16[512,128]{1,0:T(8,128)(2,1)}, bf16[512,128]{1,0:T(8,128)(2,1)}, bf16[512,128]{1,0:T(8,128)(2,1)}, bf16[128,512]{1,0:T(8,128)(2,1)}, bf16[1...) custom-call(bf16[512,128]{1,0:T(8,128)(2,1)} %x_in.1, bf16[512,128]{1,0:T(8,128)(2,1)} %k_in.1, bf16[512,512]{1,0:T(8,128)(2,1)} %a1_in.1, ...), custom_call_target="tpu_custom_call" | custom-call | tf_op jit(solution)/shard_map/mixer_layer/pallas_call | solution.py:683
  114.5 2.1 %hand_over.1 = (bf16[512,128]{1,0:T(8,128)(2,1)}, bf16[512,128]{1,0:T(8,128)(2,1)}, bf16[512,128]{1,0:T(8,128)(2,1)}, bf16[128,512]{1,0:T(8,128)(2,1)}, bf16[128...) custom-call(bf16[512,128]{1,0:T(8,128)(2,1)} %get-tuple-element.12.refs_0_, bf16[512,128]{1,0:T(8,128)(2,1)} %get-tuple-element.13.refs_1_, ...), custom_call_target="tpu_custom_call" | custom-call | tf_op jit(solution)/shard_map/hand_over/pallas_call | solution.py:694
